TPU v7x, 768 devices: a whole 4x8x12 slice. The times are simulated.
768 devices in a mesh: row: 4 (over x_lo, core), col: 192 (over z, y, x_hi).
Axes of the slice: x: 4 (x_hi: 2, x_lo: 2; x = x_hi * 2 + x_lo), y: 8, z: 12, core: 2. Of those that a mesh axis runs over, the one named last changes fastest.
Arguments:
- tokens: bfloat16 [512, 6144], P('row', 'col'), may hold values from -6 to 6
- gate_weight: bfloat16 [6144, 24576], P('row', 'col'), may hold values from -0.4375 to 0.4375
- up_weight: bfloat16 [6144, 24576], P('row', 'col'), may hold values from -0.4375 to 0.4375
- block_mask: int32 [48, 192], P(None, 'col'), may hold values from 0 to 1, as said below
- cotangent: bfloat16 [512, 24576], P('row', 'col'), may hold values from -6 to 6
Outputs:
- hidden: bfloat16 [512, 24576], P('row', 'col')
- input_grad: bfloat16 [512, 6144], P('row', 'col')
- gate_grad: float32 [6144, 24576], P('row', 'col')
- up_grad: float32 [6144, 24576], P('row', 'col')
Inputs may be any that keep to these rules, and one draw needn't show every extreme that they name: `block_mask`: in every block column, each run of 12 block rows that starts at a multiple of 12 holds exactly 6 ones, the others zero.
All inputs are finite; a program needn't handle non-finite values.
Results may differ from a plain program's by a relative error of at most 0.0085.
Values may be sent and summed in bfloat16 or wider, within the bound.
A program may use at most 32 MiB of HBM per device.

v0:
```python
import jax
import jax.numpy as jnp
from jax import lax
from jax.sharding import PartitionSpec as P

BLOCK = 128


def expand_mask(small_mask):
    return jnp.repeat(jnp.repeat(small_mask, BLOCK, axis=0), BLOCK, axis=1)


def body(tokens, gate_weight, up_weight, block_mask, cotangent):
    row_groups = lax.axis_size("row")
    row_index = lax.axis_index("row")
    seg_rows = gate_weight.shape[0]
    seg_blocks = seg_rows // BLOCK
    out_columns = gate_weight.shape[1]
    column_blocks = out_columns // BLOCK
    gathered = lax.all_gather(tokens, "col", axis=1, tiled=True)
    mask_groups = block_mask.reshape(row_groups, seg_blocks, column_blocks)
    own_mask = lax.dynamic_index_in_dim(mask_groups, row_index, 0, keepdims=False)
    own_expanded = expand_mask(own_mask).astype(jnp.bfloat16)
    gate_panel, up_panel = (
        lax.all_gather(gate_weight * own_expanded, "row", axis=0, tiled=True),
        lax.all_gather(up_weight * own_expanded, "row", axis=0, tiled=True),
    )
    gate = jnp.dot(gathered, gate_panel, preferred_element_type=jnp.float32)
    up_values = jnp.dot(gathered, up_panel, preferred_element_type=jnp.float32)
    sigmoid_gate = jax.nn.sigmoid(gate)
    silu_gate = gate * sigmoid_gate
    hidden = (silu_gate * up_values).astype(jnp.bfloat16)
    cot_float = cotangent.astype(jnp.float32)
    grad_gate = (cot_float * up_values * sigmoid_gate * (1.0 + gate * (1.0 - sigmoid_gate))).astype(
        jnp.bfloat16
    )
    grad_up = (cot_float * silu_gate).astype(jnp.bfloat16)
    contract = (((1,), (1,)), ((), ()))
    transposed = lax.psum_scatter(
        lax.dot_general(gate_panel, grad_gate, contract, preferred_element_type=jnp.float32)
        + lax.dot_general(up_panel, grad_up, contract, preferred_element_type=jnp.float32),
        "col",
        scatter_dimension=0,
        tiled=True,
    )
    input_grad = transposed.T.astype(jnp.bfloat16)
    token_contract = (((0,), (0,)), ((), ()))
    gate_partial = lax.dot_general(
        gathered, grad_gate, token_contract, preferred_element_type=jnp.float32
    )
    up_partial = lax.dot_general(
        gathered, grad_up, token_contract, preferred_element_type=jnp.float32
    )
    gate_sums, up_sums = (
        lax.psum_scatter(
            gate_partial.astype(jnp.bfloat16), "row", scatter_dimension=0, tiled=True
        ).astype(jnp.float32),
        lax.psum_scatter(
            up_partial.astype(jnp.bfloat16), "row", scatter_dimension=0, tiled=True
        ).astype(jnp.float32),
    )
    mask_float = expand_mask(own_mask).astype(jnp.float32)
    gate_grad = gate_sums * mask_float
    up_grad = up_sums * mask_float
    return (hidden, input_grad, gate_grad, up_grad)


def solution(mesh):
    placed = (P("row", "col"), P("row", "col"), P("row", "col"), P(None, "col"), P("row", "col"))
    return jax.shard_map(
        body,
        mesh=mesh,
        in_specs=placed,
        out_specs=(P("row", "col"), P("row", "col"), P("row", "col"), P("row", "col")),
        check_vma=False,
    )
```

profile of v0, /device:TPU:6, one launch (start us, length us, event | category | flops | bytes accessed | tf_op | source)
XLA Modules:
  0.0 1415.6 jit_solution(5161938672986132835)
XLA Ops:
  7.2 0.5 broadcast.23
  7.7 1.3 reduce.3
  9.2 2.3 broadcast_multiply_fusion.1
  11.6 0.7 all-gather.6.cloned.1.call-update
  12.3 0.7 all-gather.8.cloned.1.call-update
  13.1 0.1 copy.9
  13.2 37.3 %all-gather.4.cloned.1.call-done = bf16[6144,128]{1,0:T(8,128)(2,1)} async-done(((bf16[1536,128]{1,0:T(8,128)(2,1)}), bf16[6144,128]{1,0:T(8,128)(2,1)}) %all-gather.4.cloned.1.call-update) | async-done | bytes 1572880 | tf_op jit(solution)/shard_map/all_gather | solution.py:25
  50.5 176.6 %all-gather.6.cloned.1.call-done = bf16[128,6144]{0,1:T(8,128)(2,1)} async-done(((bf16[128,32]{0,1:T(8,128)(2,1)}), bf16[128,6144]{0,1:T(8,128)(2,1)}) %all-gather.6.cloned.1.call-update) | async-done | bytes 1572880 | tf_op jit(solution)/shard_map/all_gather | solution.py:20
  227.1 2.6 convolution_bitcast_fusion.1
  229.7 27.5 %all-gather.8.cloned.1.call-done = bf16[6144,128]{1,0:T(8,128)(2,1)} async-done(((bf16[1536,128]{1,0:T(8,128)(2,1)}), bf16[6144,128]{1,0:T(8,128)(2,1)}) %all-gather.8.cloned.1.call-update) | async-done | bytes 1572880 | tf_op jit(solution)/shard_map/all_gather | solution.py:26
  257.2 2.0 fusion.4
  259.3 1.7 fusion
  261.1 1.8 fusion.1
  262.9 1.3 copy-done.1
  264.2 0.5 fusion.9
  264.8 2.2 convolution_add_fusion
  267.1 0.7 copy.10
  267.8 26.4 %reduce-scatter.6.cloned.1.call-done = bf16[1536,128]{0,1:T(8,128)(2,1)} async-done(((bf16[6144,128]{0,1:T(8,128)(2,1)}), bf16[1536,128]{0,1:T(8,128)(2,1)}) %reduce-scatter.6.cloned.1.call-update) | async-done | bytes 393232 | tf_op jit(solution)/shard_map/reduce_scatter | solution.py:55
  294.2 36.1 %reduce-scatter.8.cloned.1.call-done = bf16[1536,128]{0,1:T(8,128)(2,1)} async-done(((bf16[6144,128]{0,1:T(8,128)(2,1)}), bf16[1536,128]{0,1:T(8,128)(2,1)}) %reduce-scatter.8.cloned.1.call-update) | async-done | bytes 393232 | tf_op jit(solution)/shard_map/reduce_scatter | solution.py:58
  330.3 1.3 convert_multiply_fusion
  331.6 1.2 copy.11
  332.8 1.1 copy.12
  333.9 1073.5 %reduce-scatter.4.cloned.1.call-done = f32[32,128]{1,0:T(8,128)} async-done(((f32[6144,128]{1,0:T(8,128)}), f32[32,128]{1,0:T(8,128)}) %reduce-scatter.4.cloned.1.call-update) | async-done | bytes 16400 | tf_op jit(solution)/shard_map/reduce_scatter | solution.py:39
  1407.4 1.3 convert_bitcast_fusion
  (21 shorter events, 0.6 us)
Async XLA Ops:
  7.2 5.9 copy-start.3
  7.2 43.3 %all-gather.4.cloned.1.call-start = ((), (), s32[]{:S(2)}) async-start(), calls=%async_computation.3 | async-start | bytes 1966080 | tf_op jit(solution)/shard_map/all_gather | solution.py:25
  11.5 215.6 %all-gather.6.cloned.1.call-start = ((), (), s32[]{:S(2)}) async-start(), calls=%async_computation.4 | async-start | bytes 1581056 | tf_op jit(solution)/shard_map/all_gather | solution.py:20
  12.3 245.0 %all-gather.8.cloned.1.call-start = ((), (), s32[]{:S(2)}) async-start(), calls=%async_computation.5 | async-start | bytes 1966080 | tf_op jit(solution)/shard_map/all_gather | solution.py:26
  13.0 281.2 %reduce-scatter.6.cloned.1.call-start = ((), (), s32[]{:S(2)}) async-start(), calls=%async_computation.7 | async-start | bytes 1966080 | tf_op jit(solution)/shard_map/reduce_scatter | solution.py:55
  227.1 30.1 %copy-start = (bf16[128,6144]{0,1:T(8,128)(2,1)S(1)}, bf16[128,6144]{0,1:T(8,128)(2,1)}, u32[]{:S(2)}) copy-start(bf16[128,6144]{0,1:T(8,128)(2,1)} %all-gather.6.cloned.1.call-done) | copy-start | bytes 4718596
  261.0 69.3 %reduce-scatter.8.cloned.1.call-start = ((), (), s32[]{:S(2)}) async-start(), calls=%async_computation.8 | async-start | bytes 1966080 | tf_op jit(solution)/shard_map/reduce_scatter | solution.py:58
  262.8 1.4 copy-start.1
  262.8 1.9 copy-start.2
  262.9 1144.6 %reduce-scatter.4.cloned.1.call-start = ((), (), s32[]{:S(2)}) async-start(), calls=%async_computation.6 | async-start | bytes 3162112 | tf_op jit(solution)/shard_map/reduce_scatter | solution.py:39
Sparse Core Ops, SparseCore 0:
  11.6 38.8 all-gather.3
  55.9 171.1 all-gather.5
  230.1 27.1 all-gather.7
  261.1 33.0 reduce-scatter.5
  297.2 33.0 reduce-scatter.7
  333.2 1074.1 reduce-scatter.3
where the time goes:
time: 1420 us
  waiting for transfers between devices  1380 us (97%)
    reduce_scatter x1, waiting for transfers between devices, body(): lax.psum_scatter(lax.dot_general(gate_panel, grad_gate, contract, preferr...  1070 us
    all_gather x1, waiting for transfers between devices, body(): gathered = lax.all_gather(tokens, 'col', axis=1, tiled=True)  177 us
    all_gather x1, waiting for transfers between devices, body(): lax.all_gather(gate_weight * own_expanded, 'row', axis=0, tiled=True)  37.3 us
    reduce_scatter x1, waiting for transfers between devices, body(): lax.psum_scatter(up_partial.astype(jnp.bfloat16), 'row', scatter_dimensio...  36.1 us
  transfers between devices with their start and end apart: 6, of which 6 were waited for; matrix products, arithmetic and copies ran while one was open for 1% of the time, Pallas kernels for 0%

commit v1 on v0

v1 whole, which is shorter than its diff:
```python
import functools

import jax
import jax.numpy as jnp
from jax import lax
from jax.experimental import pallas as pl
from jax.experimental.pallas import tpu as pltpu
from jax.sharding import PartitionSpec as P

MESH = pl.DeviceIdType.MESH
F32 = jnp.float32
BF16 = jnp.bfloat16
BLOCK = 128
NZ, NY, NH, ROWS = 12, 8, 2, 4
ZG = NZ // ROWS
FEATS = 32
TOK = 128
HZ, HY = NZ // 2, NY // 2
ROW_A = NY * FEATS
ROW_B = NZ * FEATS
KH = ZG * NY * FEATS
STEP_A, STEP_B = 0.65, 0.98


def ring_events(half, step, start):
    events = []
    for s in range(half):
        for direction in (0, 1):
            for chunk in (0, 1):
                if s == half - 1 and chunk != direction:
                    continue
                events.append((start + step * (2 * s + chunk), s, direction, chunk))
    return events


def sum_events(half, step, start):
    events = []
    for s in range(half):
        for direction in (0, 1):
            for chunk in (0, 1):
                if s == 0 and chunk != direction:
                    continue
                events.append((start + step * (2 * s + chunk - 1), s, direction, chunk))
    return events


def kernel(
    tok_ref, wg_ref, wu_ref, mask_ref, cot_ref,
    hid_ref, ig_ref, dg_ref, du_ref,
    own, pb, aA, aB, wcA, wcB, wtA, wtB, gsend, grecv, ggb, pA, pB,
    stA, stB, rA, rB, smA, smB, scA, scB, rsA, rsB, fin, fb,
    p0_send, p0_recv, ya_send, ya_recv, zb_send, zb_recv,
    ga_send, ga_recv, gb_send, gb_recv, x_send, x_recv, w_send, w_recv,
    sa_send, sa_recv, sb_send, sb_recv, ca_send, ca_recv, cb_send, cb_recv, f_send, f_recv,
):
    r = lax.axis_index("row")
    col = lax.axis_index("col")
    h = col % NH
    y = (col // NH) % NY
    z = col // (NH * NY)
    s_row = z // ZG
    t_z = ZG * r + z % ZG

    def at(zz, yy, hh):
        return (zz * NY + yy) * NH + hh

    def remote(src, dst, ssem, rsem, row, c):
        return pltpu.make_async_remote_copy(
            src_ref=src, dst_ref=dst, send_sem=ssem, recv_sem=rsem,
            device_id=(row, c), device_id_type=MESH,
        )

    def to_self(hh):
        return jnp.logical_and(s_row == r, h == hh)

    barrier = pltpu.get_barrier_semaphore()

    def greet(row, c):
        pl.semaphore_signal(barrier, inc=1, device_id=(row, c), device_id_type=MESH)

    for hh in range(NH):
        @pl.when(jnp.logical_not(to_self(hh)))
        def _():
            greet(s_row, at(t_z, y, hh))
    for o in range(1, NY):
        greet(r, at(z, (y + o) % NY, h))
    for o in range(1, NZ):
        greet(r, at((z + o) % NZ, y, h))
    for o in range(1, ROWS):
        greet((r + o) % ROWS, col)
    own[...] = tok_ref[...].astype(F32).T.astype(BF16)
    mirrored = jnp.where(s_row == r, NH - 1, NH)
    pl.semaphore_wait(barrier, (NY - 1) + (NZ - 1) + (ROWS - 1) + mirrored)

    def p0_copy(hh):
        return remote(own, pb.at[h], p0_send.at[hh], p0_recv.at[h], s_row, at(t_z, y, hh))

    for hh in range(NH):
        @pl.when(jnp.logical_not(to_self(hh)))
        def _():
            p0_copy(hh).start()

        @pl.when(to_self(hh))
        def _():
            pb[hh] = own[...]

    for zz in range(ZG):
        for yy in range(NY):
            keep = mask_ref[r * (ZG * NY * NH * FEATS // BLOCK) + zz * (NY * NH * FEATS // BLOCK) + yy * NH * FEATS // BLOCK, 0]
            keep = jnp.full((FEATS, BLOCK), keep.astype(F32), F32).astype(BF16)
            src = (zz * NY + yy) * NH * FEATS
            ra = (zz * NY + yy) * FEATS
            rb = (yy * ZG + zz) * FEATS
            wcA[ra:ra + FEATS, 0:128] = wg_ref[src:src + FEATS, :] * keep
            wcA[ra:ra + FEATS, 128:256] = wu_ref[src:src + FEATS, :] * keep
            wcB[rb:rb + FEATS, 0:128] = wg_ref[src + FEATS:src + 2 * FEATS, :] * keep
            wcB[rb:rb + FEATS, 128:256] = wu_ref[src + FEATS:src + 2 * FEATS, :] * keep

    for hh in range(NH):
        @pl.when(jnp.logical_not(to_self(hh)))
        def _():
            remote(own, pb.at[hh], p0_send.at[hh], p0_recv.at[hh], s_row, at(t_z, y, hh)).wait_recv()
    ya = pl.ds(pl.multiple_of(y * FEATS, FEATS), FEATS)
    zb = pl.ds(pl.multiple_of(z * FEATS, FEATS), FEATS)
    aA[z, ya, :] = pb[0]
    aB[y, zb, :] = pb[1]

    def arrived(dst, rsem, row, c):
        remote(dst, dst, p0_send.at[0], rsem, row, c).wait_recv()

    def ya_copy(o):
        return remote(pb.at[0], aA.at[z, ya], ya_send.at[o - 1], ya_recv.at[o - 1], r, at(z, (y + o) % NY, h))

    def zb_copy(o):
        return remote(pb.at[1], aB.at[y, zb], zb_send.at[o - 1], zb_recv.at[o - 1], r, at((z + o) % NZ, y, h))

    for o in (1, 7, 2, 6, 3, 5, 4):
        ya_copy(o).start()
    for o in (1, 11, 2, 10, 3, 9, 4, 8, 5, 7, 6):
        zb_copy(o).start()

    for c in range(0, KH, 256):
        wtA[:, c:c + 256] = wcA[c:c + 256, :].astype(F32).T.astype(BF16)
        wtB[:, c:c + 256] = wcB[c:c + 256, :].astype(F32).T.astype(BF16)

    def ga_copy(s, direction, chunk):
        step = s if direction == 0 else -s
        part = aA.at[(z - step + NZ) % NZ, pl.ds(chunk * (ROW_A // 2), ROW_A // 2)]
        to = (z + 1) % NZ if direction == 0 else (z + NZ - 1) % NZ
        return remote(part, part, ga_send.at[direction, s, chunk], ga_recv.at[direction, s, chunk], r, at(to, y, h))

    def gb_copy(s, direction, chunk):
        step = s if direction == 0 else -s
        part = aB.at[(y - step + NY) % NY, pl.ds(chunk * (ROW_B // 2), ROW_B // 2)]
        to = (y + 1) % NY if direction == 0 else (y + NY - 1) % NY
        return remote(part, part, gb_send.at[direction, s, chunk], gb_recv.at[direction, s, chunk], r, at(z, to, h))

    def wait_ya(o):
        frm = (y + NY - o) % NY
        arrived(aA.at[z, pl.ds(pl.multiple_of(frm * FEATS, FEATS), FEATS)], ya_recv.at[o - 1], r, at(z, frm, h))

    def wait_zb(o):
        frm = (z + NZ - o) % NZ
        arrived(aB.at[y, pl.ds(pl.multiple_of(frm * FEATS, FEATS), FEATS)], zb_recv.at[o - 1], r, at(frm, y, h))

    def wait_ga(s, direction, chunk):
        frm = (z + NZ - 1) % NZ if direction == 0 else (z + 1) % NZ
        step = s + 1 if direction == 0 else -s - 1
        part = aA.at[(z - step + NZ) % NZ, pl.ds(chunk * (ROW_A // 2), ROW_A // 2)]
        arrived(part, ga_recv.at[direction, s, chunk], r, at(frm, y, h))

    def wait_gb(s, direction, chunk):
        frm = (y + NY - 1) % NY if direction == 0 else (y + 1) % NY
        step = s + 1 if direction == 0 else -s - 1
        part = aB.at[(y - step + NY) % NY, pl.ds(chunk * (ROW_B // 2), ROW_B // 2)]
        arrived(part, gb_recv.at[direction, s, chunk], r, at(z, frm, h))

    for o in range(1, NY):
        wait_ya(o)
    order = [(t, 0, s, d, c) for t, s, d, c in ring_events(HZ, STEP_A, 0.0)]
    order += [(t, 1, s, d, c) for t, s, d, c in ring_events(HY, STEP_B, 0.5)]
    order.sort()
    arrived_b = False
    for _, which, s, d, c in order:
        if which == 1 and not arrived_b:
            arrived_b = True
            for o in range(1, NZ):
                wait_zb(o)
        if s > 0:
            (wait_ga if which == 0 else wait_gb)(s - 1, d, c)
        (ga_copy if which == 0 else gb_copy)(s, d, c).start()
    for half, wait in ((HZ, wait_ga), (HY, wait_gb)):
        wait(half - 2, 0, 1)
        wait(half - 2, 1, 0)
        wait(half - 1, 0, 0)
        wait(half - 1, 1, 1)

    def tokens_a(g):
        return aA[g * ZG:(g + 1) * ZG].reshape(KH, TOK)

    def tokens_b(g):
        return aB[:, g * ZG * FEATS:(g + 1) * ZG * FEATS, :].reshape(KH, TOK)

    for g in (0, 2):
        both = jnp.dot(wtA[...], jnp.concatenate([tokens_a(g), tokens_a(g + 1)], axis=1), preferred_element_type=F32)
        both += jnp.dot(wtB[...], jnp.concatenate([tokens_b(g), tokens_b(g + 1)], axis=1), preferred_element_type=F32)
        gsend[g] = both[:, :TOK]
        gsend[g + 1] = both[:, TOK:]

    def x_copy(o):
        g = (r + o) % ROWS
        return remote(gsend.at[g], grecv.at[o - 1], x_send.at[o - 1], x_recv.at[o - 1], g, col)

    for o in (2, 1, 3):
        x_copy(o).start()
    cot = cot_ref[...].astype(F32).T
    for o in range(1, ROWS):
        arrived(grecv.at[o - 1], x_recv.at[o - 1], (r + ROWS - o) % ROWS, col)
    total = gsend[r] + grecv[0] + grecv[1] + grecv[2]
    gate = total[:128]
    up = total[128:]
    sig = 1.0 / (1.0 + jnp.exp(-gate))
    silu = gate * sig
    ggb[r, 0:128, :] = (cot * up * sig * (1.0 + gate * (1.0 - sig))).astype(BF16)
    ggb[r, 128:256, :] = (cot * silu).astype(BF16)

    def w_copy(o):
        return remote(ggb.at[r], ggb.at[r], w_send.at[o - 1], w_recv.at[o - 1], (r + o) % ROWS, col)

    for o in (2, 1, 3):
        w_copy(o).start()
    hid_ref[...] = (silu * up).T.astype(BF16)
    for o in range(1, ROWS):
        frm = (r + ROWS - o) % ROWS
        arrived(ggb.at[frm], w_recv.at[o - 1], frm, col)

    for g in (0, 2):
        rhs = jnp.concatenate([ggb[g], ggb[g + 1]], axis=1)
        ta = jnp.dot(wcA[...], rhs, preferred_element_type=F32)
        tb = jnp.dot(wcB[...], rhs, preferred_element_type=F32)
        for k in range(2):
            lanes = slice(k * TOK, (k + 1) * TOK)
            for zz in range(ZG):
                pA[(g + k) * ZG + zz] = ta[zz * ROW_A:(zz + 1) * ROW_A, lanes]
            for yy in range(NY):
                pB[yy, (g + k) * ZG * FEATS:(g + k + 1) * ZG * FEATS, :] = tb[yy * ZG * FEATS:(yy + 1) * ZG * FEATS, lanes]

    def sum_ring(n, half, place, rows, terms, first, held, ssem, rsem, device):
        size = rows // 2

        def rows_of(chunk):
            return pl.ds(chunk * size, size)

        def copy(s, d, chunk):
            to = (place + 1) % n if d == 0 else (place + n - 1) % n
            src = first.at[d] if s == 0 else held.at[d, s - 1, rows_of(chunk)]
            return remote(src, held.at[d, s, rows_of(chunk)], ssem.at[d, s, chunk], rsem.at[d, s, chunk], r, device(to))

        def send(s, d, chunk):
            t = (place + half - s) % n if d == 0 else (place + n - half + s) % n
            mine = terms[t, rows_of(chunk), :]
            if s == 0:
                first[d] = mine.astype(BF16)
            elif s == 1 and chunk != d:
                held[d, 0, rows_of(chunk), :] = mine.astype(BF16)
            else:
                copy(s - 1, d, chunk).wait_recv()
                held[d, s - 1, rows_of(chunk), :] = (held[d, s - 1, rows_of(chunk), :].astype(F32) + mine).astype(BF16)
            copy(s, d, chunk).start()

        return copy, send

    copy_a, send_a = sum_ring(NZ, HZ, z, ROW_A, pA, stA, rA, sa_send, sa_recv, lambda to: at(to, y, h))
    copy_b, send_b = sum_ring(NY, HY, y, ROW_B, pB, stB, rB, sb_send, sb_recv, lambda to: at(z, to, h))

    def put(row, dw, keep):
        dg_ref[row:row + FEATS, :] = dw[:, :128] * keep
        du_ref[row:row + FEATS, :] = dw[:, 128:] * keep

    def keep_of(zz, yy):
        return mask_ref[r * (ZG * NY * NH * FEATS // BLOCK) + zz * (NY * NH * FEATS // BLOCK) + yy * NH * FEATS // BLOCK, 0].astype(F32)

    contract_tokens = (((1,), (1,)), ((), ()))

    def grads_a(zz):
        lhs = jnp.concatenate([aA[g * ZG + zz] for g in range(ROWS)], axis=1)
        rhs = jnp.concatenate([ggb[g] for g in range(ROWS)], axis=1)
        dw = lax.dot_general(lhs, rhs, contract_tokens, preferred_element_type=F32)
        for yy in range(NY):
            put((zz * NY + yy) * NH * FEATS, dw[yy * FEATS:(yy + 1) * FEATS], keep_of(zz, yy))

    def grads_b(yy):
        lhs = jnp.concatenate([aB[yy, g * ZG * FEATS:(g + 1) * ZG * FEATS, :] for g in range(ROWS)], axis=1)
        rhs = jnp.concatenate([ggb[g] for g in range(ROWS)], axis=1)
        dw = lax.dot_general(lhs, rhs, contract_tokens, preferred_element_type=F32)
        for zz in range(ZG):
            put(((zz * NY + yy) * NH + 1) * FEATS, dw[zz * FEATS:(zz + 1) * FEATS], keep_of(zz, yy))

    pieces = [functools.partial(grads_a, zz) for zz in range(ZG)] + [functools.partial(grads_b, yy) for yy in range(NY)]
    order = [(t, 0, s, d, c) for t, s, d, c in sum_events(HZ, STEP_A, 0.0)]
    order += [(t, 1, s, d, c) for t, s, d, c in sum_events(HY, STEP_B, 0.1)]
    order.sort()
    sent = 0
    for _, which, s, d, c in order:
        (send_a if which == 0 else send_b)(s, d, c)
        sent += 1
        if sent >= 4 and sent % 3 == 1 and pieces:
            pieces.pop(0)()
    while pieces:
        pieces.pop(0)()

    def ca_copy(o):
        to = (y + o) % NY
        src = scA.at[pl.ds(pl.multiple_of(to * FEATS, FEATS), FEATS)]
        return remote(src, rsA.at[o - 1], ca_send.at[o - 1], ca_recv.at[o - 1], r, at(z, to, h))

    def cb_copy(o):
        to = (z + o) % NZ
        src = scB.at[pl.ds(pl.multiple_of(to * FEATS, FEATS), FEATS)]
        return remote(src, rsB.at[o - 1], cb_send.at[o - 1], cb_recv.at[o - 1], r, at(to, y, h))

    def last_sum(half, place, terms, held, sums, rounded, copy, size):
        for c in range(2):
            rows = slice(c * size, (c + 1) * size)
            for d in range(2):
                copy(half - 1, d, c).wait_recv()
            whole = terms[place, rows, :] + held[0, half - 1, rows, :].astype(F32) + held[1, half - 1, rows, :].astype(F32)
            sums[rows, :] = whole
            rounded[rows, :] = whole.astype(BF16)

    last_sum(HZ, z, pA, rA, smA, scA, copy_a, ROW_A // 2)
    for o in (4, 3, 5, 2, 6, 1, 7):
        ca_copy(o).start()
    last_sum(HY, y, pB, rB, smB, scB, copy_b, ROW_B // 2)
    for o in (6, 5, 7, 4, 8, 3, 9, 2, 10, 1, 11):
        cb_copy(o).start()

    def f_copy(hh):
        return remote(fin.at[hh], fb.at[h], f_send.at[hh], f_recv.at[h], s_row, at(t_z, y, hh))

    whole = smA[ya, :]
    for o in range(1, NY):
        ca_copy(o).wait_recv()
        whole += rsA[o - 1].astype(F32)
    fin[0] = whole
    whole = smB[zb, :]
    for o in range(1, NZ):
        cb_copy(o).wait_recv()
        whole += rsB[o - 1].astype(F32)
    fin[1] = whole
    for hh in range(NH):
        @pl.when(jnp.logical_not(to_self(hh)))
        def _():
            f_copy(hh).start()

        @pl.when(to_self(hh))
        def _():
            fb[hh] = fin[hh]

    for o in range(1, NY):
        ya_copy(o).wait_send()
        ca_copy(o).wait_send()
    for o in range(1, NZ):
        zb_copy(o).wait_send()
        cb_copy(o).wait_send()
    for o in range(1, ROWS):
        x_copy(o).wait_send()
        w_copy(o).wait_send()
    for _, s, d, c in ring_events(HZ, 1.0, 0.0):
        ga_copy(s, d, c).wait_send()
    for _, s, d, c in ring_events(HY, 1.0, 0.0):
        gb_copy(s, d, c).wait_send()
    for _, s, d, c in sum_events(HZ, 1.0, 0.0):
        copy_a(s, d, c).wait_send()
    for _, s, d, c in sum_events(HY, 1.0, 0.0):
        copy_b(s, d, c).wait_send()
    for hh in range(NH):
        @pl.when(jnp.logical_not(to_self(hh)))
        def _():
            p0_copy(hh).wait_send()
            f_copy(hh).wait_send()
            remote(fin.at[hh], fb.at[hh], f_send.at[hh], f_recv.at[hh], s_row, at(t_z, y, hh)).wait_recv()
    ig_ref[...] = (fb[0] + fb[1]).T.astype(BF16)


def body(tokens, gate_weight, up_weight, block_mask, cotangent):
    vmem = pl.BlockSpec(memory_space=pltpu.VMEM)
    dma = pltpu.SemaphoreType.DMA
    return pl.pallas_call(
        kernel,
        out_shape=(
            jax.ShapeDtypeStruct(cotangent.shape, BF16),
            jax.ShapeDtypeStruct(tokens.shape, BF16),
            jax.ShapeDtypeStruct(gate_weight.shape, F32),
            jax.ShapeDtypeStruct(up_weight.shape, F32),
        ),
        in_specs=[vmem, vmem, vmem, pl.BlockSpec(memory_space=pltpu.SMEM), vmem],
        out_specs=(vmem,) * 4,
        scratch_shapes=[
            pltpu.VMEM((FEATS, TOK), BF16),
            pltpu.VMEM((NH, FEATS, TOK), BF16),
            pltpu.VMEM((NZ, ROW_A, TOK), BF16),
            pltpu.VMEM((NY, ROW_B, TOK), BF16),
            pltpu.VMEM((KH, 256), BF16),
            pltpu.VMEM((KH, 256), BF16),
            pltpu.VMEM((256, KH), BF16),
            pltpu.VMEM((256, KH), BF16),
            pltpu.VMEM((ROWS, 256, TOK), F32),
            pltpu.VMEM((ROWS - 1, 256, TOK), F32),
            pltpu.VMEM((ROWS, 256, TOK), BF16),
            pltpu.VMEM((NZ, ROW_A, TOK), F32),
            pltpu.VMEM((NY, ROW_B, TOK), F32),
            pltpu.VMEM((2, ROW_A // 2, TOK), BF16),
            pltpu.VMEM((2, ROW_B // 2, TOK), BF16),
            pltpu.VMEM((2, HZ, ROW_A, TOK), BF16),
            pltpu.VMEM((2, HY, ROW_B, TOK), BF16),
            pltpu.VMEM((ROW_A, TOK), F32),
            pltpu.VMEM((ROW_B, TOK), F32),
            pltpu.VMEM((ROW_A, TOK), BF16),
            pltpu.VMEM((ROW_B, TOK), BF16),
            pltpu.VMEM((NY - 1, FEATS, TOK), BF16),
            pltpu.VMEM((NZ - 1, FEATS, TOK), BF16),
            pltpu.VMEM((NH, FEATS, TOK), F32),
            pltpu.VMEM((NH, FEATS, TOK), F32),
            dma((NH,)), dma((NH,)),
            dma((NY - 1,)), dma((NY - 1,)), dma((NZ - 1,)), dma((NZ - 1,)),
            dma((2, HZ, 2)), dma((2, HZ, 2)), dma((2, HY, 2)), dma((2, HY, 2)),
            dma((ROWS - 1,)), dma((ROWS - 1,)), dma((ROWS - 1,)), dma((ROWS - 1,)),
            dma((2, HZ, 2)), dma((2, HZ, 2)), dma((2, HY, 2)), dma((2, HY, 2)),
            dma((NY - 1,)), dma((NY - 1,)), dma((NZ - 1,)), dma((NZ - 1,)),
            dma((NH,)), dma((NH,)),
        ],
        compiler_params=pltpu.CompilerParams(
            collective_id=0, has_side_effects=True, vmem_limit_bytes=40 << 20
        ),
    )(tokens, gate_weight, up_weight, block_mask, cotangent)


def solution(mesh):
    placed = (P("row", "col"), P("row", "col"), P("row", "col"), P(None, "col"), P("row", "col"))
    return jax.shard_map(
        body,
        mesh=mesh,
        in_specs=placed,
        out_specs=(P("row", "col"), P("row", "col"), P("row", "col"), P("row", "col")),
        check_vma=False,
    )
```

time: 1420 us -> 107 us (0.08)
  waiting for transfers between devices: 1380 us -> 0 us
  Pallas kernels: 0 us -> 98.9 us
    reduce_scatter x3 -> x0, waiting for transfers between devices: 1140 us -> none  [the longest x1 1070 us: body(): lax.psum_scatter(lax.dot_general(gate_panel, grad_gate, contract, preferr...]
    all_gather x3 -> x0, waiting for transfers between devices: 241 us -> none  [the longest x1 177 us: body(): gathered = lax.all_gather(tokens, 'col', axis=1, tiled=True)]
    pallas_call x0 -> x1, Pallas kernels: none -> 98.9 us  [body(): pl.pallas_call(kernel, out_shape=(jax.ShapeDtypeStruct(cotangent.shape, B...]
  transfers between devices with their start and end apart: 6 -> 0, of which waited for: 6 -> 0; matrix products, arithmetic and copies ran while one was open for 1% -> 0% of each run, Pallas kernels for 0% -> 0%
where the time goes in v1:
time: 107 us; the launch traced here: 106 us
  Pallas kernels  98.9 us (92%)
  local copies, waits for them, and re-layouts  6.6 us (6%)
    pallas_call x1, Pallas kernels, body(): pl.pallas_call(kernel, out_shape=(jax.ShapeDtypeStruct(cotangent.shape, B...  98.9 us
    unnamed x11, local copies, waits for them, and re-layouts  5.92 us

profile of v1, /device:TPU:6, one launch (start us, length us, event | category | flops | bytes accessed | tf_op | source)
XLA Modules:
  0.0 106.2 jit_solution(15357542075519819284)
XLA Ops:
  0.6 0.0 copy-start.2
  0.6 0.7 copy.10.mask_ref
  1.4 0.8 copy.9.tok_ref
  2.2 0.0 copy-done.2
  2.2 0.0 copy-start
  2.2 1.0 copy-done
  3.2 0.0 copy-start.1
  3.2 1.0 copy-done.1
  4.2 98.9 %shard_map.84 = (bf16[128,128]{1,0:T(8,128)(2,1)S(1)}, bf16[128,32]{1,0:T(8,128)(2,1)S(1)}, f32[1536,128]{1,0:T(8,128)S(1)}, f32[1536,128]{1,0:T(8,128)S(1)}) custom-call(bf16[128,32]{1,0:T(8,128)(2,1)S(1)} %copy.9.tok_ref, bf16[1536,128]{1,0:T(8,128)(2,1)S(1)} %copy-done, bf16[1536,128]{1,0:T(8,128)(2,1)S(1)} %copy-done.1, s32[48,1]{1,0:T(8,128)S(1)} %copy.10.mask_ref, ...), custom_call_target="tpu_custom_call" | custom-call | tf_op jit(solution)/shard_map/pallas_call | solution.py:389
  103.2 0.7 copy.11
  103.8 0.6 copy.15
  104.4 0.9 copy.16
  105.3 0.9 copy.17
Async XLA Ops:
  0.6 1.6 %copy-start.2 = (bf16[128,128]{1,0:T(8,128)(2,1)S(1)}, bf16[128,128]{1,0:T(8,128)(2,1)}, u32[]{:S(2)}) copy-start(bf16[128,128]{1,0:T(8,128)(2,1)} %cot_ref.1) | copy-start | bytes 98308
  2.2 1.0 copy-start
  3.2 1.0 copy-start.1

commit v2 on v1

v2 whole, which is shorter than its diff:
```python
import functools

import jax
import jax.numpy as jnp
from jax import lax
from jax.experimental import pallas as pl
from jax.experimental.pallas import tpu as pltpu
from jax.sharding import PartitionSpec as P

MESH = pl.DeviceIdType.MESH
F32 = jnp.float32
BF16 = jnp.bfloat16
BLOCK = 128
NZ, NY, NH, ROWS = 12, 8, 2, 4
ZG = NZ // ROWS
FEATS = 32
TOK = 128
SEGB = ZG * NY * NH * FEATS // BLOCK
HZ, HY = NZ // 2, NY // 2
ROW_A = NY * FEATS
ROW_B = NZ * FEATS
GROUP_B = ZG * FEATS
FAR_Y = (4, 3, 5, 2, 6, 1, 7)
FAR_Z = (6, 5, 7, 4, 8, 3, 9, 2, 10, 1, 11)
STEP_A, STEP_B = 0.65, 0.98


def ring_events(half, step, start):
    events = []
    for s in range(half):
        for direction in (0, 1):
            for chunk in (0, 1):
                if s == half - 1 and chunk != direction:
                    continue
                events.append((start + step * (2 * s + chunk), s, direction, chunk))
    return events


def sum_events(half, step, start):
    events = []
    for s in range(half):
        for direction in (0, 1):
            for chunk in (0, 1):
                if s == 0 and chunk != direction:
                    continue
                events.append((start + step * (2 * s + chunk - 1), s, direction, chunk))
    return events


def kernel(
    own, wg_hbm, wu_hbm, mask_ref, cot_hbm,
    hid_ref, ig_ref, dg_ref, du_ref,
    wg_ref, wu_ref, cot_ref, load_sem, pb, aA, aB, wA, wB, gg, ggT, dA, dB, qA, qB,
    stA, stB, rA, rB, smA, smB, scA, scB, rsA, rsB, fin, fb,
    h_send, h_recv, ya_send, ya_recv, zb_send, zb_recv, ga_send, ga_recv, gb_send, gb_recv,
    w_send, w_recv, d_send, d_recv,
    sa_send, sa_recv, sb_send, sb_recv, ca_send, ca_recv, cb_send, cb_recv,
):
    r = lax.axis_index("row")
    col = lax.axis_index("col")
    h = col % NH
    y = (col // NH) % NY
    z = col // (NH * NY)
    sibling = r + 1 - 2 * (r % 2)
    across = (r + 2) % ROWS
    diagonal = (sibling + 2) % ROWS

    def at(zz, yy, hh):
        return (zz * NY + yy) * NH + hh

    def remote(src, dst, ssem, rsem, row, c):
        return pltpu.make_async_remote_copy(
            src_ref=src, dst_ref=dst, send_sem=ssem, recv_sem=rsem,
            device_id=(row, c), device_id_type=MESH,
        )

    sent = []

    def go(copy):
        copy.start()
        sent.append(copy)

    def arrived(dst, rsem, row, c):
        remote(dst, dst, h_send.at[0], rsem, row, c).wait_recv()

    loads = [
        pltpu.make_async_copy(src, dst, load_sem.at[i])
        for i, (src, dst) in enumerate(((wg_hbm, wg_ref), (wu_hbm, wu_ref), (cot_hbm, cot_ref)))
    ]

    barrier = pltpu.get_barrier_semaphore()

    def greet(row, c):
        pl.semaphore_signal(barrier, inc=1, device_id=(row, c), device_id_type=MESH)

    for o in FAR_Z:
        greet(r, at((z + o) % NZ, y, h))
    for o in FAR_Y:
        greet(r, at(z, (y + o) % NY, h))
    partner = at(z, y, 1 - h)
    greet(r, partner)
    greet(across, col)
    greet(sibling, col)
    for load in loads:
        load.start()
    pl.semaphore_wait(barrier, (NY - 1) + (NZ - 1) + 3)

    go(remote(own, pb.at[h], h_send.at[0], h_recv.at[0], r, partner))
    pb[h] = own[...]

    def keep_of(zz, yy):
        return mask_ref[0, r * SEGB + zz * (SEGB // ZG) + yy * NH * FEATS // BLOCK].astype(F32)

    loads[0].wait()
    loads[1].wait()
    for zz in range(ZG):
        for yy in range(NY):
            keep = jnp.full((FEATS, BLOCK), keep_of(zz, yy), F32).astype(BF16)
            src = (zz * NY + yy) * NH * FEATS
            ra = slice(yy * FEATS, (yy + 1) * FEATS)
            rb = pl.ds(pl.multiple_of(r * GROUP_B + zz * FEATS, FEATS), FEATS)
            wA[r * ZG + zz, ra, 0:128] = wg_ref[src:src + FEATS, :] * keep
            wA[r * ZG + zz, ra, 128:256] = wu_ref[src:src + FEATS, :] * keep
            wB[yy, rb, 0:128] = wg_ref[src + FEATS:src + 2 * FEATS, :] * keep
            wB[yy, rb, 128:256] = wu_ref[src + FEATS:src + 2 * FEATS, :] * keep

    def weights_of(row):
        return (
            wA.at[pl.ds(row * ZG, ZG)],
            wB.at[:, pl.ds(pl.multiple_of(row * GROUP_B, FEATS), GROUP_B)],
        )

    def hand(which, owner, row):
        for part in range(2):
            ref = weights_of(owner)[part]
            go(remote(ref, ref, w_send.at[which, part], w_recv.at[which, part], row, col))

    def handed(which, owner, row):
        for part in range(2):
            arrived(weights_of(owner)[part], w_recv.at[which, part], row, col)

    hand(1, r, across)
    hand(0, r, sibling)

    arrived(pb.at[1 - h], h_recv.at[0], r, partner)
    ya = pl.ds(pl.multiple_of(y * FEATS, FEATS), FEATS)
    zb = pl.ds(pl.multiple_of(z * FEATS, FEATS), FEATS)

    def ya_copy(o):
        return remote(pb.at[0], aA.at[z, ya], ya_send.at[o - 1], ya_recv.at[o - 1], r, at(z, (y + o) % NY, h))

    def zb_copy(o):
        return remote(pb.at[1], aB.at[y, zb], zb_send.at[o - 1], zb_recv.at[o - 1], r, at((z + o) % NZ, y, h))

    for o in FAR_Y:
        go(ya_copy(o))
    for o in FAR_Z:
        go(zb_copy(o))
    aA[z, ya, :] = pb[0]
    aB[y, zb, :] = pb[1]

    def ga_copy(s, direction, chunk):
        step = s if direction == 0 else -s
        part = aA.at[(z - step + NZ) % NZ, pl.ds(chunk * (ROW_A // 2), ROW_A // 2)]
        to = (z + 1) % NZ if direction == 0 else (z + NZ - 1) % NZ
        return remote(part, part, ga_send.at[direction, s, chunk], ga_recv.at[direction, s, chunk], r, at(to, y, h))

    def gb_copy(s, direction, chunk):
        step = s if direction == 0 else -s
        part = aB.at[(y - step + NY) % NY, pl.ds(chunk * (ROW_B // 2), ROW_B // 2)]
        to = (y + 1) % NY if direction == 0 else (y + NY - 1) % NY
        return remote(part, part, gb_send.at[direction, s, chunk], gb_recv.at[direction, s, chunk], r, at(z, to, h))

    def wait_ya(o):
        frm = (y + NY - o) % NY
        arrived(aA.at[z, pl.ds(pl.multiple_of(frm * FEATS, FEATS), FEATS)], ya_recv.at[o - 1], r, at(z, frm, h))

    def wait_zb(o):
        frm = (z + NZ - o) % NZ
        arrived(aB.at[y, pl.ds(pl.multiple_of(frm * FEATS, FEATS), FEATS)], zb_recv.at[o - 1], r, at(frm, y, h))

    def wait_ga(s, direction, chunk):
        frm = (z + NZ - 1) % NZ if direction == 0 else (z + 1) % NZ
        step = s + 1 if direction == 0 else -s - 1
        part = aA.at[(z - step + NZ) % NZ, pl.ds(chunk * (ROW_A // 2), ROW_A // 2)]
        arrived(part, ga_recv.at[direction, s, chunk], r, at(frm, y, h))

    def wait_gb(s, direction, chunk):
        frm = (y + NY - 1) % NY if direction == 0 else (y + 1) % NY
        step = s + 1 if direction == 0 else -s - 1
        part = aB.at[(y - step + NY) % NY, pl.ds(chunk * (ROW_B // 2), ROW_B // 2)]
        arrived(part, gb_recv.at[direction, s, chunk], r, at(z, frm, h))

    for o in range(1, NY):
        wait_ya(o)
    order = [(t, 0, s, d, c) for t, s, d, c in ring_events(HZ, STEP_A, 0.0)]
    order += [(t, 1, s, d, c) for t, s, d, c in ring_events(HY, STEP_B, 0.5)]
    order.sort()
    arrived_b = False
    for _, which, s, d, c in order:
        if which == 1 and not arrived_b:
            arrived_b = True
            for o in range(1, NZ):
                wait_zb(o)
        if s > 0:
            (wait_ga if which == 0 else wait_gb)(s - 1, d, c)
        go((ga_copy if which == 0 else gb_copy)(s, d, c))
    handed(1, across, across)
    hand(2, across, sibling)
    for half, wait in ((HZ, wait_ga), (HY, wait_gb)):
        wait(half - 2, 0, 1)
        wait(half - 2, 1, 0)
        wait(half - 1, 0, 0)
        wait(half - 1, 1, 1)

    handed(0, sibling, sibling)
    handed(2, diagonal, sibling)

    over_features = (((0,), (0,)), ((), ()))
    both = jnp.zeros((TOK, 256), F32)
    for zz in range(NZ):
        both += lax.dot_general(aA[zz], wA[zz], over_features, preferred_element_type=F32)
    for yy in range(NY):
        both += lax.dot_general(aB[yy], wB[yy], over_features, preferred_element_type=F32)
    gate = both[:, :128]
    up = both[:, 128:]
    loads[2].wait()
    cot = cot_ref[...].astype(F32)
    sig = 1.0 / (1.0 + jnp.exp(-gate))
    silu = gate * sig
    grad_gate = cot * up * sig * (1.0 + gate * (1.0 - sig))
    grad_up = cot * silu
    ggT[0:128, :] = grad_gate.T.astype(BF16)
    ggT[128:256, :] = grad_up.T.astype(BF16)
    gg[:, 0:128] = grad_gate.astype(BF16)
    gg[:, 128:256] = grad_up.astype(BF16)
    hid_ref[...] = (silu * up).astype(BF16)

    def sum_ring(n, half, place, rows, weights, first, held, ssem, rsem, device):
        size = rows // 2

        def rows_of(chunk):
            return pl.ds(chunk * size, size)

        def copy(s, d, chunk):
            to = (place + 1) % n if d == 0 else (place + n - 1) % n
            src = first.at[d] if s == 0 else held.at[d, s - 1, rows_of(chunk)]
            return remote(src, held.at[d, s, rows_of(chunk)], ssem.at[d, s, chunk], rsem.at[d, s, chunk], r, device(to))

        def send(s, d, chunk):
            t = (place + half - s) % n if d == 0 else (place + n - half + s) % n
            mine = jnp.dot(weights[t, rows_of(chunk), :], ggT[...], preferred_element_type=F32)
            if s == 0:
                first[d] = mine.astype(BF16)
            elif s == 1 and chunk != d:
                held[d, 0, rows_of(chunk), :] = mine.astype(BF16)
            else:
                copy(s - 1, d, chunk).wait_recv()
                held[d, s - 1, rows_of(chunk), :] = (held[d, s - 1, rows_of(chunk), :].astype(F32) + mine).astype(BF16)
            go(copy(s, d, chunk))

        return copy, send

    copy_a, send_a = sum_ring(NZ, HZ, z, ROW_A, wA, stA, rA, sa_send, sa_recv, lambda to: at(to, y, h))
    copy_b, send_b = sum_ring(NY, HY, y, ROW_B, wB, stB, rB, sb_send, sb_recv, lambda to: at(z, to, h))

    owners = (r, sibling, across, diagonal)

    def grads_a(i):
        for zz in range(ZG):
            dA[i, zz] = jnp.dot(aA[owners[i] * ZG + zz], gg[...], preferred_element_type=F32).astype(BF16)

    def grads_b(i, some):
        rows = pl.ds(pl.multiple_of(owners[i] * GROUP_B, FEATS), GROUP_B)
        for yy in some:
            dB[i, yy] = jnp.dot(aB[yy, rows, :], gg[...], preferred_element_type=F32).astype(BF16)

    def pass_on(i, slot, part, row):
        src, dst = ((dA, qA), (dB, qB))[part]
        go(remote(src.at[i], dst.at[slot], d_send.at[slot, part], d_recv.at[slot, part], row, col))

    def got(slot, part, row):
        dst = (qA, qB)[part]
        arrived(dst.at[slot], d_recv.at[slot, part], row, col)

    def add_sibling(part):
        got(1, part, sibling)
        mine, other = ((dA, qA), (dB, qB))[part]
        for k in range(mine.shape[1]):
            mine[2, k] = (mine[2, k].astype(F32) + other[1, k].astype(F32)).astype(BF16)
        pass_on(2, 2, part, across)

    low, high = range(NY // 2), range(NY // 2, NY)
    pieces = []
    for i, slot in ((3, 1), (2, None), (1, 0), (0, None)):
        pieces.append(functools.partial(grads_a, i))
        if slot is not None:
            pieces.append(functools.partial(pass_on, i, slot, 0, sibling))
        pieces += [functools.partial(grads_b, i, low), functools.partial(grads_b, i, high)]
        if slot is not None:
            pieces.append(functools.partial(pass_on, i, slot, 1, sibling))
        if i == 2:
            pieces += [functools.partial(add_sibling, 0), functools.partial(add_sibling, 1)]
    order = [(t, 0, s, d, c) for t, s, d, c in sum_events(HZ, STEP_A, 0.0)]
    order += [(t, 1, s, d, c) for t, s, d, c in sum_events(HY, STEP_B, 0.1)]
    order.sort()
    count = 0
    for _, which, s, d, c in order:
        (send_a if which == 0 else send_b)(s, d, c)
        count += 1
        if count >= 4 and pieces:
            pieces.pop(0)()
    while pieces:
        pieces.pop(0)()

    def ca_copy(o):
        to = (y + o) % NY
        src = scA.at[pl.ds(pl.multiple_of(to * FEATS, FEATS), FEATS)]
        return remote(src, rsA.at[o - 1], ca_send.at[o - 1], ca_recv.at[o - 1], r, at(z, to, h))

    def cb_copy(o):
        to = (z + o) % NZ
        src = scB.at[pl.ds(pl.multiple_of(to * FEATS, FEATS), FEATS)]
        return remote(src, rsB.at[o - 1], cb_send.at[o - 1], cb_recv.at[o - 1], r, at(to, y, h))

    def last_sum(half, place, weights, held, sums, rounded, copy, size):
        for c in range(2):
            rows = slice(c * size, (c + 1) * size)
            whole = jnp.dot(weights[place, rows, :], ggT[...], preferred_element_type=F32)
            for d in range(2):
                copy(half - 1, d, c).wait_recv()
            whole += held[0, half - 1, rows, :].astype(F32) + held[1, half - 1, rows, :].astype(F32)
            sums[rows, :] = whole
            rounded[rows, :] = whole.astype(BF16)

    last_sum(HZ, z, wA, rA, smA, scA, copy_a, ROW_A // 2)
    for o in FAR_Y:
        go(ca_copy(o))
    last_sum(HY, y, wB, rB, smB, scB, copy_b, ROW_B // 2)
    for o in FAR_Z:
        go(cb_copy(o))

    whole = smA[ya, :]
    for o in range(1, NY):
        ca_copy(o).wait_recv()
        whole += rsA[o - 1].astype(F32)
    fin[0] = whole
    whole = smB[zb, :]
    for o in range(1, NZ):
        cb_copy(o).wait_recv()
        whole += rsB[o - 1].astype(F32)
    fin[1] = whole
    go(remote(fin.at[1 - h], fb, h_send.at[1], h_recv.at[1], r, partner))

    def put(row, dw, keep):
        dg_ref[row:row + FEATS, :] = dw[:, :128] * keep
        du_ref[row:row + FEATS, :] = dw[:, 128:] * keep

    got(0, 0, sibling)
    got(2, 0, across)
    for zz in range(ZG):
        for yy in range(NY):
            rows = slice(yy * FEATS, (yy + 1) * FEATS)
            dw = dA[0, zz, rows, :].astype(F32) + qA[0, zz, rows, :].astype(F32) + qA[2, zz, rows, :].astype(F32)
            put((zz * NY + yy) * NH * FEATS, dw, keep_of(zz, yy))
    got(0, 1, sibling)
    got(2, 1, across)
    for yy in range(NY):
        for zz in range(ZG):
            rows = slice(zz * FEATS, (zz + 1) * FEATS)
            dw = dB[0, yy, rows, :].astype(F32) + qB[0, yy, rows, :].astype(F32) + qB[2, yy, rows, :].astype(F32)
            put(((zz * NY + yy) * NH + 1) * FEATS, dw, keep_of(zz, yy))

    arrived(fb, h_recv.at[1], r, partner)
    ig_ref[...] = (fin[h] + fb[...]).astype(BF16)
    for copy in sent:
        copy.wait_send()


def body(tokens, gate_weight, up_weight, block_mask, cotangent):
    vmem = pl.BlockSpec(memory_space=pltpu.VMEM)
    dma = pltpu.SemaphoreType.DMA
    hbm = pl.BlockSpec(memory_space=pltpu.HBM)
    hidden, input_grad, gate_grad, up_grad = pl.pallas_call(
        kernel,
        out_shape=(
            jax.ShapeDtypeStruct(cotangent.shape, BF16),
            jax.ShapeDtypeStruct(tokens.shape[::-1], BF16),
            jax.ShapeDtypeStruct(gate_weight.shape, F32),
            jax.ShapeDtypeStruct(up_weight.shape, F32),
        ),
        in_specs=[vmem, hbm, hbm, pl.BlockSpec(memory_space=pltpu.SMEM), hbm],
        out_specs=(vmem,) * 4,
        scratch_shapes=[
            pltpu.VMEM(gate_weight.shape, BF16),
            pltpu.VMEM(up_weight.shape, BF16),
            pltpu.VMEM(cotangent.shape, BF16),
            dma((3,)),
            pltpu.VMEM((NH, FEATS, TOK), BF16),
            pltpu.VMEM((NZ, ROW_A, TOK), BF16),
            pltpu.VMEM((NY, ROW_B, TOK), BF16),
            pltpu.VMEM((NZ, ROW_A, 256), BF16),
            pltpu.VMEM((NY, ROW_B, 256), BF16),
            pltpu.VMEM((TOK, 256), BF16),
            pltpu.VMEM((256, TOK), BF16),
            pltpu.VMEM((ROWS, ZG, ROW_A, 256), BF16),
            pltpu.VMEM((ROWS, NY, GROUP_B, 256), BF16),
            pltpu.VMEM((3, ZG, ROW_A, 256), BF16),
            pltpu.VMEM((3, NY, GROUP_B, 256), BF16),
            pltpu.VMEM((2, ROW_A // 2, TOK), BF16),
            pltpu.VMEM((2, ROW_B // 2, TOK), BF16),
            pltpu.VMEM((2, HZ, ROW_A, TOK), BF16),
            pltpu.VMEM((2, HY, ROW_B, TOK), BF16),
            pltpu.VMEM((ROW_A, TOK), F32),
            pltpu.VMEM((ROW_B, TOK), F32),
            pltpu.VMEM((ROW_A, TOK), BF16),
            pltpu.VMEM((ROW_B, TOK), BF16),
            pltpu.VMEM((NY - 1, FEATS, TOK), BF16),
            pltpu.VMEM((NZ - 1, FEATS, TOK), BF16),
            pltpu.VMEM((NH, FEATS, TOK), F32),
            pltpu.VMEM((FEATS, TOK), F32),
            dma((2,)), dma((2,)),
            dma((NY - 1,)), dma((NY - 1,)), dma((NZ - 1,)), dma((NZ - 1,)),
            dma((2, HZ, 2)), dma((2, HZ, 2)), dma((2, HY, 2)), dma((2, HY, 2)),
            dma((3, 2)), dma((3, 2)), dma((3, 2)), dma((3, 2)),
            dma((2, HZ, 2)), dma((2, HZ, 2)), dma((2, HY, 2)), dma((2, HY, 2)),
            dma((NY - 1,)), dma((NY - 1,)), dma((NZ - 1,)), dma((NZ - 1,)),
        ],
        compiler_params=pltpu.CompilerParams(
            collective_id=0, has_side_effects=True, vmem_limit_bytes=40 << 20
        ),
    )(tokens.T, gate_weight, up_weight, block_mask.T, cotangent)
    return hidden, input_grad.T, gate_grad, up_grad


def solution(mesh):
    placed = (P("row", "col"), P("row", "col"), P("row", "col"), P(None, "col"), P("row", "col"))
    return jax.shard_map(
        body,
        mesh=mesh,
        in_specs=placed,
        out_specs=(P("row", "col"), P("row", "col"), P("row", "col"), P("row", "col")),
        check_vma=False,
    )
```

time: 107 us -> 91.6 us (0.86)
  Pallas kernels: 98.9 us -> 83.4 us
    pallas_call x1, Pallas kernels: 98.9 us -> 83.4 us  [body(): pl.pallas_call(kernel, out_shape=(jax.ShapeDtypeStruct(cotangent.shape, B...]
    unnamed x11 -> x14, local copies, waits for them, and re-layouts: 5.92 us -> 7.07 us
where the time goes in v2:
time: 91.6 us; the launch traced here: 91.1 us
  Pallas kernels  83.4 us (91%)
  local copies, waits for them, and re-layouts  7.07 us (8%)
    pallas_call x1, Pallas kernels, body(): pl.pallas_call(kernel, out_shape=(jax.ShapeDtypeStruct(cotangent.shape, B...  83.4 us
    unnamed x14, local copies, waits for them, and re-layouts  7.07 us

profile of v2, /device:TPU:6, one launch (start us, length us, event | category | flops | bytes accessed | tf_op | source)
XLA Modules:
  0.0 91.1 jit_solution(6697722163666042862)
XLA Ops:
  0.6 0.0 copy-start.4
  0.6 0.6 copy-done.4
  1.3 0.0 copy-start
  1.3 1.0 %copy-done = bf16[1536,128]{1,0:T(8,128)(2,1)S(1)} copy-done((bf16[1536,128]{1,0:T(8,128)(2,1)S(1)}, bf16[1536,128]{1,0:T(8,128)(2,1)}, u32[]{:S(2)}) %copy-start) | copy-done | bytes 393240
  2.3 0.0 copy-start.1
  2.3 1.0 %copy-done.1 = bf16[1536,128]{1,0:T(8,128)(2,1)S(1)} copy-done((bf16[1536,128]{1,0:T(8,128)(2,1)S(1)}, bf16[1536,128]{1,0:T(8,128)(2,1)}, u32[]{:S(2)}) %copy-start.1) | copy-done | bytes 393240
  3.3 0.0 copy-start.2
  3.3 0.8 copy-done.2
  4.0 0.0 copy-start.3
  4.0 0.7 copy-done.3
  4.7 83.4 %shard_map.84 = (bf16[128,128]{1,0:T(8,128)(2,1)S(1)}, bf16[32,128]{1,0:T(8,128)(2,1)S(1)}, f32[1536,128]{1,0:T(8,128)S(1)}, f32[1536,128]{1,0:T(8,128)S(1)}) custom-call(bf16[32,128]{1,0:T(8,128)(2,1)S(1)} %bitcast.3, bf16[1536,128]{1,0:T(8,128)(2,1)S(1)} %copy-done, bf16[1536,128]{1,0:T(8,128)(2,1)S(1)} %copy-done.1, s32[1,48]{1,0:T(1,128)S(1)} %bitcast.5, ...), custom_call_target="tpu_custom_call" | custom-call | tf_op jit(solution)/shard_map/pallas_call | solution.py:384
  88.1 0.6 copy.13
  88.8 0.6 copy.14
  89.4 0.9 copy.15
  90.2 0.9 copy.16
Async XLA Ops:
  0.6 0.7 copy-start.4
  1.3 1.0 %copy-start = (bf16[1536,128]{1,0:T(8,128)(2,1)S(1)}, bf16[1536,128]{1,0:T(8,128)(2,1)}, u32[]{:S(2)}) copy-start(bf16[1536,128]{1,0:T(8,128)(2,1)} %wg_hbm.1) | copy-start | bytes 1179652
  2.3 1.0 %copy-start.1 = (bf16[1536,128]{1,0:T(8,128)(2,1)S(1)}, bf16[1536,128]{1,0:T(8,128)(2,1)}, u32[]{:S(2)}) copy-start(bf16[1536,128]{1,0:T(8,128)(2,1)} %wu_hbm.1) | copy-start | bytes 1179652
  3.3 0.8 copy-start.2
  4.0 0.7 copy-start.3

commit v3 on v2

v3 whole, which is shorter than its diff:
```python
import functools

import jax
import jax.numpy as jnp
from jax import lax
from jax.experimental import pallas as pl
from jax.experimental.pallas import tpu as pltpu
from jax.sharding import PartitionSpec as P

MESH = pl.DeviceIdType.MESH
F32 = jnp.float32
BF16 = jnp.bfloat16
BLOCK = 128
NZ, NY, NH, ROWS = 12, 8, 2, 4
ZG = NZ // ROWS
FEATS = 32
TOK = 128
SEGB = ZG * NY * NH * FEATS // BLOCK
QY = NY // 2
ROW_A = NY * FEATS
ROW_B = NZ * FEATS
GROUP_B = ZG * FEATS
FAR_Y = (4, 3, 5, 2, 6, 1, 7)
FAR_Z = (6, 5, 7, 4, 8, 3, 9, 2, 10, 1, 11)


def kernel(
    own, wg_hbm, wu_hbm, mask_ref, cot_hbm,
    hid_ref, ig_ref, dg_ref, du_ref,
    wg_ref, wu_ref, cot_ref, load_sem, pb, aA, aB, wA, wB, gg, ggT, dA, dB, qA, qB,
    s1A, s1B, t1A, t1B, u1A, u1B, v1A, v1B, t2A, t2B, v2A, v2B, t3A, t3B, fin, fb,
    h_send, h_recv, w_send, w_recv, d_send, d_recv,
    a1_send, a1_recv, a2_send, a2_recv, a3_send, a3_recv, b1_send, b1_recv, b2_send, b2_recv, b3_send, b3_recv,
    ra1_send, ra1_recv, ra2_send, ra2_recv, ra3_send, ra3_recv,
    rb1_send, rb1_recv, rb2_send, rb2_recv, rb3_send, rb3_recv,
):
    r = lax.axis_index("row")
    col = lax.axis_index("col")
    h = col % NH
    y = (col // NH) % NY
    z = col // (NH * NY)
    k, m = z // ZG, z % ZG
    j, q = y // QY, y % QY
    sibling = r + 1 - 2 * (r % 2)
    across = (r + 2) % ROWS
    diagonal = (sibling + 2) % ROWS

    def at(zz, yy, hh):
        return (zz * NY + yy) * NH + hh

    def remote(src, dst, ssem, rsem, row, c):
        return pltpu.make_async_remote_copy(
            src_ref=src, dst_ref=dst, send_sem=ssem, recv_sem=rsem,
            device_id=(row, c), device_id_type=MESH,
        )

    sent = []

    def go(copy):
        copy.start()
        sent.append(copy)

    def arrived(dst, rsem, row, c):
        remote(dst, dst, h_send.at[0], rsem, row, c).wait_recv()

    loads = [
        pltpu.make_async_copy(src, dst, load_sem.at[i])
        for i, (src, dst) in enumerate(((wg_hbm, wg_ref), (wu_hbm, wu_ref), (cot_hbm, cot_ref)))
    ]

    barrier = pltpu.get_barrier_semaphore()

    def greet(row, c):
        pl.semaphore_signal(barrier, inc=1, device_id=(row, c), device_id_type=MESH)

    for o in FAR_Z:
        greet(r, at((z + o) % NZ, y, h))
    for o in FAR_Y:
        greet(r, at(z, (y + o) % NY, h))
    partner = at(z, y, 1 - h)
    greet(r, partner)
    greet(across, col)
    greet(sibling, col)
    for load in loads:
        load.start()
    pl.semaphore_wait(barrier, (NY - 1) + (NZ - 1) + 3)

    go(remote(own, pb.at[h], h_send.at[0], h_recv.at[0], r, partner))
    pb[h] = own[...]

    def keep_of(zz, yy):
        return mask_ref[0, r * SEGB + zz * (SEGB // ZG) + yy * NH * FEATS // BLOCK].astype(F32)

    loads[0].wait()
    loads[1].wait()
    for zz in range(ZG):
        for yy in range(NY):
            keep = jnp.full((FEATS, BLOCK), keep_of(zz, yy), F32).astype(BF16)
            src = (zz * NY + yy) * NH * FEATS
            ra = slice(yy * FEATS, (yy + 1) * FEATS)
            rb = pl.ds(pl.multiple_of(r * GROUP_B + zz * FEATS, FEATS), FEATS)
            wA[r, zz, ra, 0:128] = wg_ref[src:src + FEATS, :] * keep
            wA[r, zz, ra, 128:256] = wu_ref[src:src + FEATS, :] * keep
            wB[yy // QY, yy % QY, rb, 0:128] = wg_ref[src + FEATS:src + 2 * FEATS, :] * keep
            wB[yy // QY, yy % QY, rb, 128:256] = wu_ref[src + FEATS:src + 2 * FEATS, :] * keep

    def weights_of(row):
        return (
            wA.at[row],
            wB.at[:, :, pl.ds(pl.multiple_of(row * GROUP_B, FEATS), GROUP_B)],
        )

    def hand(which, owner, row):
        for part in range(2):
            ref = weights_of(owner)[part]
            go(remote(ref, ref, w_send.at[which, part], w_recv.at[which, part], row, col))

    def handed(which, owner, row):
        for part in range(2):
            arrived(weights_of(owner)[part], w_recv.at[which, part], row, col)

    hand(1, r, across)
    hand(0, r, sibling)

    arrived(pb.at[1 - h], h_recv.at[0], r, partner)
    ya = pl.ds(pl.multiple_of(y * FEATS, FEATS), FEATS)
    zb = pl.ds(pl.multiple_of(z * FEATS, FEATS), FEATS)

    def a1_copy(o):
        slot = aA.at[k, m, ya]
        return remote(pb.at[0], slot, a1_send.at[o - 1], a1_recv.at[o - 1], r, at((z + ZG * o) % NZ, y, h))

    def b1_copy():
        return remote(pb.at[1], aB.at[j, q, zb], b1_send.at[0], b1_recv.at[0], r, at(z, (y + QY) % NY, h))

    def a2_copy(o):
        part = aA.at[:, m, ya]
        return remote(part, part, a2_send.at[o - 1], a2_recv.at[o - 1], r, at(z, (y + o) % NY, h))

    def b2_copy(o):
        part = aB.at[:, q, zb]
        return remote(part, part, b2_send.at[o - 1], b2_recv.at[o - 1], r, at((z + o) % NZ, y, h))

    z_next, z_last = (z + 1) % NZ, (z + NZ - 1) % NZ
    y_next, y_last, y_next2, y_last2 = (y + 1) % NY, (y + NY - 1) % NY, (y + 2) % NY, (y + NY - 2) % NY
    m_next, m_last = (m + 1) % ZG, (m + ZG - 1) % ZG
    q_next, q_last, q_far = (q + 1) % QY, (q + QY - 1) % QY, (q + 2) % QY

    def a3_copy(d, i):
        part = aA.at[i, m]
        return remote(part, part, a3_send.at[d, i], a3_recv.at[d, i], r, at((z_next, z_last)[d], y, h))

    def b3_copy(d, i):
        part = aB.at[i, q]
        to = ((y_next, y_last)[d] if d < 2 else (y_next2, y_last2)[i])
        return remote(part, part, b3_send.at[d, i], b3_recv.at[d, i], r, at(z, to, h))

    for o in (2, 1, 3):
        go(a1_copy(o))
    go(b1_copy())
    aA[k, m, ya, :] = pb[0]
    aB[j, q, zb, :] = pb[1]
    arrived(aB.at[1 - j, q, zb], b1_recv.at[0], r, at(z, (y + QY) % NY, h))
    for o in FAR_Z:
        go(b2_copy(o))
    for o in range(1, ROWS):
        frm = (z + NZ - ZG * o) % NZ
        arrived(aA.at[frm // ZG, m, ya], a1_recv.at[o - 1], r, at(frm, y, h))
    for o in FAR_Y:
        go(a2_copy(o))
    for o in FAR_Y[::-1]:
        frm = (y + NY - o) % NY
        rows = pl.ds(pl.multiple_of(frm * FEATS, FEATS), FEATS)
        arrived(aA.at[:, m, rows], a2_recv.at[o - 1], r, at(z, frm, h))
    for i in range(ROWS):
        for d in range(2):
            go(a3_copy(d, i))
    for o in FAR_Z[::-1]:
        frm = (z + NZ - o) % NZ
        rows = pl.ds(pl.multiple_of(frm * FEATS, FEATS), FEATS)
        arrived(aB.at[:, q, rows], b2_recv.at[o - 1], r, at(frm, y, h))
    for d, i in ((2, 0), (2, 1), (0, 0), (1, 0), (0, 1), (1, 1)):
        go(b3_copy(d, i))
    handed(1, across, across)
    hand(2, across, sibling)
    for i in range(ROWS):
        for d in range(2):
            arrived(aA.at[i, (m_last, m_next)[d]], a3_recv.at[d, i], r, at((z_last, z_next)[d], y, h))
    for d, i in ((2, 0), (2, 1), (0, 0), (1, 0), (0, 1), (1, 1)):
        part = aB.at[i, (q_last, q_next, q_far)[d]]
        frm = ((y_last, y_next)[d] if d < 2 else (y_last2, y_next2)[i])
        arrived(part, b3_recv.at[d, i], r, at(z, frm, h))
    handed(0, sibling, sibling)
    handed(2, diagonal, sibling)

    over_features = (((0,), (0,)), ((), ()))
    both = jnp.zeros((TOK, 256), F32)
    for zz in range(NZ):
        at_z = (zz // ZG, zz % ZG)
        both += lax.dot_general(aA[at_z], wA[at_z], over_features, preferred_element_type=F32)
    for yy in range(NY):
        at_y = (yy // QY, yy % QY)
        both += lax.dot_general(aB[at_y], wB[at_y], over_features, preferred_element_type=F32)
    gate = both[:, :128]
    up = both[:, 128:]
    loads[2].wait()
    cot = cot_ref[...].astype(F32)
    sig = 1.0 / (1.0 + jnp.exp(-gate))
    silu = gate * sig
    grad_gate = cot * up * sig * (1.0 + gate * (1.0 - sig))
    grad_up = cot * silu
    ggT[0:128, :] = grad_gate.T.astype(BF16)
    ggT[128:256, :] = grad_up.T.astype(BF16)
    gg[:, 0:128] = grad_gate.astype(BF16)
    gg[:, 128:256] = grad_up.astype(BF16)
    hid_ref[...] = (silu * up).astype(BF16)

    def terms(weights):
        return jnp.dot(weights, ggT[...], preferred_element_type=F32)

    def ra1_copy(d, i):
        return remote(s1A.at[d, i], t1A.at[d, i], ra1_send.at[d, i], ra1_recv.at[d, i], r, at((z_next, z_last)[d], y, h))

    def rb1_copy(d, i):
        to = ((y_next, y_last)[d] if d < 2 else (y_next2, y_last2)[i])
        return remote(s1B.at[d, i], t1B.at[d, i], rb1_send.at[d, i], rb1_recv.at[d, i], r, at(z, to, h))

    def ra2_copy(o):
        to = (y + o) % NY
        src = v1A.at[:, pl.ds(pl.multiple_of(to * FEATS, FEATS), FEATS)]
        return remote(src, t2A.at[o - 1], ra2_send.at[o - 1], ra2_recv.at[o - 1], r, at(z, to, h))

    def rb2_copy(o):
        to = (z + o) % NZ
        src = v1B.at[:, pl.ds(pl.multiple_of(to * FEATS, FEATS), FEATS)]
        return remote(src, t2B.at[o - 1], rb2_send.at[o - 1], rb2_recv.at[o - 1], r, at(to, y, h))

    def ra3_copy(o):
        to = (z + ZG * o) % NZ
        return remote(v2A.at[to // ZG], t3A.at[o - 1], ra3_send.at[o - 1], ra3_recv.at[o - 1], r, at(to, y, h))

    def rb3_copy():
        return remote(v2B.at[1 - j], t3B, rb3_send.at[0], rb3_recv.at[0], r, at(z, (y + QY) % NY, h))

    for i in range(2):
        s1B[2, i] = terms(wB[i, q_far]).astype(BF16)
        go(rb1_copy(2, i))
        for d in range(2):
            s1A[d, i] = terms(wA[i, (m_next, m_last)[d]]).astype(BF16)
            go(ra1_copy(d, i))
    for i in range(2):
        for d in range(2):
            s1B[d, i] = terms(wB[i, (q_next, q_last)[d]]).astype(BF16)
            go(rb1_copy(d, i))
            s1A[d, 2 + i] = terms(wA[2 + i, (m_next, m_last)[d]]).astype(BF16)
            go(ra1_copy(d, 2 + i))

    owners = (r, sibling, across, diagonal)

    def grads_a(i):
        for zz in range(ZG):
            dA[i, zz] = jnp.dot(aA[owners[i], zz], gg[...], preferred_element_type=F32).astype(BF16)

    def grads_b(i, some):
        rows = pl.ds(pl.multiple_of(owners[i] * GROUP_B, FEATS), GROUP_B)
        for yy in some:
            dB[i, yy] = jnp.dot(aB[yy // QY, yy % QY, rows, :], gg[...], preferred_element_type=F32).astype(BF16)

    def pass_on(i, slot, part, row):
        src, dst = ((dA, qA), (dB, qB))[part]
        go(remote(src.at[i], dst.at[slot], d_send.at[slot, part], d_recv.at[slot, part], row, col))

    def got(slot, part, row):
        dst = (qA, qB)[part]
        arrived(dst.at[slot], d_recv.at[slot, part], row, col)

    def add_sibling(part):
        got(1, part, sibling)
        mine, other = ((dA, qA), (dB, qB))[part]
        for i in range(mine.shape[1]):
            mine[2, i] = (mine[2, i].astype(F32) + other[1, i].astype(F32)).astype(BF16)
        pass_on(2, 2, part, across)

    every = range(NY)
    for i, slot in ((3, 1), (2, None)):
        grads_a(i)
        if slot is not None:
            pass_on(i, slot, 0, sibling)
        grads_b(i, every)
        if slot is not None:
            pass_on(i, slot, 1, sibling)
    for i in range(ROWS):
        u1A[i] = terms(wA[i, m])
    for i in range(2):
        u1B[i] = terms(wB[i, q])
    add_sibling(0)
    add_sibling(1)

    for i in range(ROWS):
        for d in range(2):
            ra1_copy(d, i).wait_recv()
        total = u1A[i] + t1A[0, i].astype(F32) + t1A[1, i].astype(F32)
        u1A[i] = total
        v1A[i] = total.astype(BF16)
    for o in FAR_Y:
        go(ra2_copy(o))
    for i in range(2):
        for d in (2, 0, 1):
            rb1_copy(d, i).wait_recv()
        total = u1B[i] + t1B[0, i].astype(F32) + t1B[1, i].astype(F32) + t1B[2, i].astype(F32)
        u1B[i] = total
        v1B[i] = total.astype(BF16)
    for o in FAR_Z:
        go(rb2_copy(o))

    grads_a(1)
    pass_on(1, 0, 0, sibling)
    grads_b(1, every)
    pass_on(1, 0, 1, sibling)

    total = u1A[:, ya, :]
    for o in FAR_Y[::-1]:
        ra2_copy(o).wait_recv()
        total += t2A[o - 1].astype(F32)
    v2A[...] = total.astype(BF16)
    fin[0:ROWS] = total
    for o in (2, 1, 3):
        go(ra3_copy(o))
    total = u1B[:, zb, :]
    for o in FAR_Z[::-1]:
        rb2_copy(o).wait_recv()
        total += t2B[o - 1].astype(F32)
    v2B[...] = total.astype(BF16)
    fin[ROWS:ROWS + 2] = total
    go(rb3_copy())

    grads_a(0)
    grads_b(0, every)

    total = fin[k]
    for o in (1, 3, 2):
        ra3_copy(o).wait_recv()
        total += t3A[o - 1].astype(F32)
    fin[ROWS + 2] = total
    rb3_copy().wait_recv()
    fin[ROWS + 3] = fin[ROWS + j] + t3B[...].astype(F32)
    go(remote(fin.at[ROWS + 3 - h], fb, h_send.at[1], h_recv.at[1], r, partner))

    def put(row, dw, keep):
        dg_ref[row:row + FEATS, :] = dw[:, :128] * keep
        du_ref[row:row + FEATS, :] = dw[:, 128:] * keep

    got(0, 0, sibling)
    got(2, 0, across)
    for zz in range(ZG):
        for yy in range(NY):
            rows = slice(yy * FEATS, (yy + 1) * FEATS)
            dw = dA[0, zz, rows, :].astype(F32) + qA[0, zz, rows, :].astype(F32) + qA[2, zz, rows, :].astype(F32)
            put((zz * NY + yy) * NH * FEATS, dw, keep_of(zz, yy))
    got(0, 1, sibling)
    got(2, 1, across)
    for yy in range(NY):
        for zz in range(ZG):
            rows = slice(zz * FEATS, (zz + 1) * FEATS)
            dw = dB[0, yy, rows, :].astype(F32) + qB[0, yy, rows, :].astype(F32) + qB[2, yy, rows, :].astype(F32)
            put(((zz * NY + yy) * NH + 1) * FEATS, dw, keep_of(zz, yy))

    arrived(fb, h_recv.at[1], r, partner)
    ig_ref[...] = (fin[ROWS + 2 + h] + fb[...]).astype(BF16)
    for copy in sent:
        copy.wait_send()


def body(tokens, gate_weight, up_weight, block_mask, cotangent):
    vmem = pl.BlockSpec(memory_space=pltpu.VMEM)
    dma = pltpu.SemaphoreType.DMA
    hbm = pl.BlockSpec(memory_space=pltpu.HBM)
    hidden, input_grad, gate_grad, up_grad = pl.pallas_call(
        kernel,
        out_shape=(
            jax.ShapeDtypeStruct(cotangent.shape, BF16),
            jax.ShapeDtypeStruct(tokens.shape[::-1], BF16),
            jax.ShapeDtypeStruct(gate_weight.shape, F32),
            jax.ShapeDtypeStruct(up_weight.shape, F32),
        ),
        in_specs=[vmem, hbm, hbm, pl.BlockSpec(memory_space=pltpu.SMEM), hbm],
        out_specs=(vmem,) * 4,
        scratch_shapes=[
            pltpu.VMEM(gate_weight.shape, BF16),
            pltpu.VMEM(up_weight.shape, BF16),
            pltpu.VMEM(cotangent.shape, BF16),
            dma((3,)),
            pltpu.VMEM((NH, FEATS, TOK), BF16),
            pltpu.VMEM((ROWS, ZG, ROW_A, TOK), BF16),
            pltpu.VMEM((2, QY, ROW_B, TOK), BF16),
            pltpu.VMEM((ROWS, ZG, ROW_A, 256), BF16),
            pltpu.VMEM((2, QY, ROW_B, 256), BF16),
            pltpu.VMEM((TOK, 256), BF16),
            pltpu.VMEM((256, TOK), BF16),
            pltpu.VMEM((ROWS, ZG, ROW_A, 256), BF16),
            pltpu.VMEM((ROWS, NY, GROUP_B, 256), BF16),
            pltpu.VMEM((3, ZG, ROW_A, 256), BF16),
            pltpu.VMEM((3, NY, GROUP_B, 256), BF16),
            pltpu.VMEM((2, ROWS, ROW_A, TOK), BF16),
            pltpu.VMEM((3, 2, ROW_B, TOK), BF16),
            pltpu.VMEM((2, ROWS, ROW_A, TOK), BF16),
            pltpu.VMEM((3, 2, ROW_B, TOK), BF16),
            pltpu.VMEM((ROWS, ROW_A, TOK), F32),
            pltpu.VMEM((2, ROW_B, TOK), F32),
            pltpu.VMEM((ROWS, ROW_A, TOK), BF16),
            pltpu.VMEM((2, ROW_B, TOK), BF16),
            pltpu.VMEM((NY - 1, ROWS, FEATS, TOK), BF16),
            pltpu.VMEM((NZ - 1, 2, FEATS, TOK), BF16),
            pltpu.VMEM((ROWS, FEATS, TOK), BF16),
            pltpu.VMEM((2, FEATS, TOK), BF16),
            pltpu.VMEM((ROWS - 1, FEATS, TOK), BF16),
            pltpu.VMEM((FEATS, TOK), BF16),
            pltpu.VMEM((ROWS + 4, FEATS, TOK), F32),
            pltpu.VMEM((FEATS, TOK), F32),
            dma((2,)), dma((2,)), dma((3, 2)), dma((3, 2)), dma((3, 2)), dma((3, 2)),
            *[dma(n) for n in ((ROWS - 1,), (NY - 1,), (2, ROWS), (1,), (NZ - 1,), (3, 2)) for _ in range(2)],
            *[dma(n) for n in ((2, ROWS), (NY - 1,), (ROWS - 1,), (3, 2), (NZ - 1,), (1,)) for _ in range(2)],
        ],
        compiler_params=pltpu.CompilerParams(
            collective_id=0, has_side_effects=True, vmem_limit_bytes=40 << 20
        ),
    )(tokens.T, gate_weight, up_weight, block_mask.T, cotangent)
    return hidden, input_grad.T, gate_grad, up_grad


def solution(mesh):
    placed = (P("row", "col"), P("row", "col"), P("row", "col"), P(None, "col"), P("row", "col"))
    return jax.shard_map(
        body,
        mesh=mesh,
        in_specs=placed,
        out_specs=(P("row", "col"), P("row", "col"), P("row", "col"), P("row", "col")),
        check_vma=False,
    )
```

time: 91.6 us -> 80.6 us (0.88)
  the two profiles are of different devices: /device:TPU:6 before, /device:TPU:8 now
where the time goes in v3:
time: 80.6 us; the launch traced here: 80.2 us
  Pallas kernels  72.5 us (90%)
  local copies, waits for them, and re-layouts  7.07 us (9%)
    pallas_call x1, Pallas kernels, body(): pl.pallas_call(kernel, out_shape=(jax.ShapeDtypeStruct(cotangent.shape, B...  72.5 us
    unnamed x14, local copies, waits for them, and re-layouts  7.07 us

profile of v3, /device:TPU:8, one launch (start us, length us, event | category | flops | bytes accessed | tf_op | source)
XLA Modules:
  0.0 80.2 jit_solution(1284115245425836211)
XLA Ops:
  0.6 0.0 copy-start.4
  0.6 0.6 copy-done.4
  1.3 0.0 copy-start
  1.3 1.0 %copy-done = bf16[1536,128]{1,0:T(8,128)(2,1)S(1)} copy-done((bf16[1536,128]{1,0:T(8,128)(2,1)S(1)}, bf16[1536,128]{1,0:T(8,128)(2,1)}, u32[]{:S(2)}) %copy-start) | copy-done | bytes 393240
  2.3 0.0 copy-start.1
  2.3 1.0 %copy-done.1 = bf16[1536,128]{1,0:T(8,128)(2,1)S(1)} copy-done((bf16[1536,128]{1,0:T(8,128)(2,1)S(1)}, bf16[1536,128]{1,0:T(8,128)(2,1)}, u32[]{:S(2)}) %copy-start.1) | copy-done | bytes 393240
  3.3 0.0 copy-start.2
  3.3 0.8 copy-done.2
  4.0 0.0 copy-start.3
  4.0 0.7 copy-done.3
  4.7 72.5 %shard_map.84 = (bf16[128,128]{1,0:T(8,128)(2,1)S(1)}, bf16[32,128]{1,0:T(8,128)(2,1)S(1)}, f32[1536,128]{1,0:T(8,128)S(1)}, f32[1536,128]{1,0:T(8,128)S(1)}) custom-call(bf16[32,128]{1,0:T(8,128)(2,1)S(1)} %bitcast.3, bf16[1536,128]{1,0:T(8,128)(2,1)S(1)} %copy-done, bf16[1536,128]{1,0:T(8,128)(2,1)S(1)} %copy-done.1, s32[1,48]{1,0:T(1,128)S(1)} %bitcast.5, ...), custom_call_target="tpu_custom_call" | custom-call | tf_op jit(solution)/shard_map/pallas_call | solution.py:378
  77.3 0.6 copy.13
  77.9 0.6 copy.14
  78.5 0.9 %copy.15 = f32[1536,128]{1,0:T(8,128)} copy(f32[1536,128]{1,0:T(8,128)S(1)} %get-tuple-element.18) | data formatting | bytes 1572864
  79.4 0.9 %copy.16 = f32[1536,128]{1,0:T(8,128)} copy(f32[1536,128]{1,0:T(8,128)S(1)} %get-tuple-element.19) | data formatting | bytes 1572864
Async XLA Ops:
  0.6 0.7 copy-start.4
  1.3 1.0 %copy-start = (bf16[1536,128]{1,0:T(8,128)(2,1)S(1)}, bf16[1536,128]{1,0:T(8,128)(2,1)}, u32[]{:S(2)}) copy-start(bf16[1536,128]{1,0:T(8,128)(2,1)} %wg_hbm.1) | copy-start | bytes 1179652
  2.3 1.0 %copy-start.1 = (bf16[1536,128]{1,0:T(8,128)(2,1)S(1)}, bf16[1536,128]{1,0:T(8,128)(2,1)}, u32[]{:S(2)}) copy-start(bf16[1536,128]{1,0:T(8,128)(2,1)} %wu_hbm.1) | copy-start | bytes 1179652
  3.3 0.8 copy-start.2
  4.0 0.7 copy-start.3

commit v4 on v3

--- a/solution.py
+++ b/solution.py
@@ -26,10 +26,10 @@
 
 def kernel(
     own, wg_hbm, wu_hbm, mask_ref, cot_hbm,
-    hid_ref, ig_ref, dg_ref, du_ref,
-    wg_ref, wu_ref, cot_ref, load_sem, pb, aA, aB, wA, wB, gg, ggT, dA, dB, qA, qB,
-    s1A, s1B, t1A, t1B, u1A, u1B, v1A, v1B, t2A, t2B, v2A, v2B, t3A, t3B, fin, fb,
-    h_send, h_recv, w_send, w_recv, d_send, d_recv,
+    hid_hbm, ig_ref, dg_hbm, du_hbm,
+    hid_ref, dg_ref, du_ref, store_sem, wg_ref, wu_ref, cot_ref, load_sem, aA, aB, wA, wB, gg, ggT, dA, dB, qA, qB,
+    s1A, s1B, t1A, t1B, u1A, u1B, v1A, v1B, t2A, t2B, v2A, v2B, t3A, t3B, fin,
+    w_send, w_recv, d_send, d_recv,
     a1_send, a1_recv, a2_send, a2_recv, a3_send, a3_recv, b1_send, b1_recv, b2_send, b2_recv, b3_send, b3_recv,
     ra1_send, ra1_recv, ra2_send, ra2_recv, ra3_send, ra3_recv,
     rb1_send, rb1_recv, rb2_send, rb2_recv, rb3_send, rb3_recv,
@@ -61,7 +61,7 @@
         sent.append(copy)
 
     def arrived(dst, rsem, row, c):
-        remote(dst, dst, h_send.at[0], rsem, row, c).wait_recv()
+        remote(dst, dst, w_send.at[0, 0], rsem, row, c).wait_recv()
 
     loads = [
         pltpu.make_async_copy(src, dst, load_sem.at[i])
@@ -77,16 +77,40 @@
         greet(r, at((z + o) % NZ, y, h))
     for o in FAR_Y:
         greet(r, at(z, (y + o) % NY, h))
-    partner = at(z, y, 1 - h)
-    greet(r, partner)
+    for o in (2, 1, 3, 0):
+        greet(r, at((z + ZG * o) % NZ, y, 1 - h))
+    greet(r, at(z, (y + QY) % NY, 1 - h))
     greet(across, col)
     greet(sibling, col)
     for load in loads:
         load.start()
-    pl.semaphore_wait(barrier, (NY - 1) + (NZ - 1) + 3)
-
-    go(remote(own, pb.at[h], h_send.at[0], h_recv.at[0], r, partner))
-    pb[h] = own[...]
+    pl.semaphore_wait(barrier, (NY - 1) + (NZ - 1) + 7)
+
+    ya = pl.ds(pl.multiple_of(y * FEATS, FEATS), FEATS)
+    zb = pl.ds(pl.multiple_of(z * FEATS, FEATS), FEATS)
+
+    def a1_copy(o, hh):
+        return remote(own, aA.at[k, m, ya], a1_send.at[o, hh], a1_recv.at[o], r, at((z + ZG * o) % NZ, y, hh))
+
+    def b1_copy(e, hh):
+        return remote(own, aB.at[j, q, zb], b1_send.at[e, hh], b1_recv.at[e], r, at(z, (y + QY * e) % NY, hh))
+
+    def first_round(plane):
+        if plane:
+            return [b1_copy(e, hh) for e, hh in ((1, 0), (1, 1), (0, 0))]
+        return [a1_copy(o, hh) for o, hh in ((2, 1), (2, 0), (1, 1), (3, 1), (1, 0), (3, 0), (0, 1))]
+
+    @pl.when(h == 0)
+    def _():
+        for copy in first_round(0):
+            copy.start()
+        aA[k, m, ya, :] = own[...]
+
+    @pl.when(h == 1)
+    def _():
+        for copy in first_round(1):
+            copy.start()
+        aB[j, q, zb, :] = own[...]
 
     def keep_of(zz, yy):
         return mask_ref[0, r * SEGB + zz * (SEGB // ZG) + yy * NH * FEATS // BLOCK].astype(F32)
@@ -122,17 +146,6 @@
     hand(1, r, across)
     hand(0, r, sibling)
 
-    arrived(pb.at[1 - h], h_recv.at[0], r, partner)
-    ya = pl.ds(pl.multiple_of(y * FEATS, FEATS), FEATS)
-    zb = pl.ds(pl.multiple_of(z * FEATS, FEATS), FEATS)
-
-    def a1_copy(o):
-        slot = aA.at[k, m, ya]
-        return remote(pb.at[0], slot, a1_send.at[o - 1], a1_recv.at[o - 1], r, at((z + ZG * o) % NZ, y, h))
-
-    def b1_copy():
-        return remote(pb.at[1], aB.at[j, q, zb], b1_send.at[0], b1_recv.at[0], r, at(z, (y + QY) % NY, h))
-
     def a2_copy(o):
         part = aA.at[:, m, ya]
         return remote(part, part, a2_send.at[o - 1], a2_recv.at[o - 1], r, at(z, (y + o) % NY, h))
@@ -146,50 +159,67 @@
     m_next, m_last = (m + 1) % ZG, (m + ZG - 1) % ZG
     q_next, q_last, q_far = (q + 1) % QY, (q + QY - 1) % QY, (q + 2) % QY
 
-    def a3_copy(d, i):
-        part = aA.at[i, m]
-        return remote(part, part, a3_send.at[d, i], a3_recv.at[d, i], r, at((z_next, z_last)[d], y, h))
-
-    def b3_copy(d, i):
-        part = aB.at[i, q]
-        to = ((y_next, y_last)[d] if d < 2 else (y_next2, y_last2)[i])
-        return remote(part, part, b3_send.at[d, i], b3_recv.at[d, i], r, at(z, to, h))
-
-    for o in (2, 1, 3):
-        go(a1_copy(o))
-    go(b1_copy())
-    aA[k, m, ya, :] = pb[0]
-    aB[j, q, zb, :] = pb[1]
-    arrived(aB.at[1 - j, q, zb], b1_recv.at[0], r, at(z, (y + QY) % NY, h))
+    def group_a(g):
+        return pl.ds(pl.multiple_of((j + g) % 2 * (QY * FEATS), FEATS), QY * FEATS)
+
+    def group_b(g):
+        return pl.ds(pl.multiple_of((k + g) % ROWS * GROUP_B, FEATS), GROUP_B)
+
+    y_to = (y_next, y_last, y_next2, y_last2)
+    y_from = (y_last, y_next, y_last2, y_next2)
+
+    def a3_copy(d, g):
+        part = aA.at[:, m, group_a(g)]
+        return remote(part, part, a3_send.at[d, g], a3_recv.at[d, g], r, at((z_next, z_last)[d], y, h))
+
+    def b3_copy(d, g):
+        part = aB.at[:, q, group_b(g)] if d < 2 else aB.at[d - 2, q, group_b(g)]
+        return remote(part, part, b3_send.at[d, g], b3_recv.at[d, g], r, at(z, y_to[d], h))
+
+    def wait_a2(g):
+        for t in range(1 - g, QY):
+            frm = (j + g) % 2 * QY + (q + t) % QY
+            rows = pl.ds(pl.multiple_of(frm * FEATS, FEATS), FEATS)
+            arrived(aA.at[:, m, rows], a2_recv.at[(y + NY - frm) % NY - 1], r, at(z, frm, h))
+
+    def wait_b2(g):
+        for t in range(0 if g else 1, ZG):
+            frm = (k + g) % ROWS * ZG + (m + t) % ZG
+            rows = pl.ds(pl.multiple_of(frm * FEATS, FEATS), FEATS)
+            arrived(aB.at[:, q, rows], b2_recv.at[(z + NZ - frm) % NZ - 1], r, at(frm, y, h))
+
+    arrived(aB.at[1 - j, q, zb], b1_recv.at[1], r, at(z, (y + QY) % NY, 1))
+
+    @pl.when(h == 0)
+    def _():
+        arrived(aB.at[j, q, zb], b1_recv.at[0], r, at(z, y, 1))
+
     for o in FAR_Z:
         go(b2_copy(o))
     for o in range(1, ROWS):
         frm = (z + NZ - ZG * o) % NZ
-        arrived(aA.at[frm // ZG, m, ya], a1_recv.at[o - 1], r, at(frm, y, h))
+        arrived(aA.at[frm // ZG, m, ya], a1_recv.at[o], r, at(frm, y, 0))
+
+    @pl.when(h == 1)
+    def _():
+        arrived(aA.at[k, m, ya], a1_recv.at[0], r, at(z, y, 0))
+
     for o in FAR_Y:
         go(a2_copy(o))
-    for o in FAR_Y[::-1]:
-        frm = (y + NY - o) % NY
-        rows = pl.ds(pl.multiple_of(frm * FEATS, FEATS), FEATS)
-        arrived(aA.at[:, m, rows], a2_recv.at[o - 1], r, at(z, frm, h))
-    for i in range(ROWS):
-        for d in range(2):
-            go(a3_copy(d, i))
-    for o in FAR_Z[::-1]:
-        frm = (z + NZ - o) % NZ
-        rows = pl.ds(pl.multiple_of(frm * FEATS, FEATS), FEATS)
-        arrived(aB.at[:, q, rows], b2_recv.at[o - 1], r, at(frm, y, h))
-    for d, i in ((2, 0), (2, 1), (0, 0), (1, 0), (0, 1), (1, 1)):
-        go(b3_copy(d, i))
+    for half, g in ((0, 0), (1, 0), (1, 1), (1, 3), (0, 1), (1, 2)):
+        (wait_b2 if half else wait_a2)(g)
+        for d in (2, 3, 0, 1) if half else (0, 1):
+            go((b3_copy if half else a3_copy)(d, g))
     handed(1, across, across)
     hand(2, across, sibling)
-    for i in range(ROWS):
-        for d in range(2):
-            arrived(aA.at[i, (m_last, m_next)[d]], a3_recv.at[d, i], r, at((z_last, z_next)[d], y, h))
-    for d, i in ((2, 0), (2, 1), (0, 0), (1, 0), (0, 1), (1, 1)):
-        part = aB.at[i, (q_last, q_next, q_far)[d]]
-        frm = ((y_last, y_next)[d] if d < 2 else (y_last2, y_next2)[i])
-        arrived(part, b3_recv.at[d, i], r, at(z, frm, h))
+    for half, g in ((0, 0), (1, 0), (1, 1), (1, 3), (0, 1), (1, 2)):
+        for d in (2, 3, 0, 1) if half else (0, 1):
+            if half:
+                cls = (q_last, q_next, q_far, q_far)[d]
+                part = aB.at[:, cls, group_b(g)] if d < 2 else aB.at[d - 2, cls, group_b(g)]
+                arrived(part, b3_recv.at[d, g], r, at(z, y_from[d], h))
+            else:
+                arrived(aA.at[:, (m_last, m_next)[d], group_a(g)], a3_recv.at[d, g], r, at((z_last, z_next)[d], y, h))
     handed(0, sibling, sibling)
     handed(2, diagonal, sibling)
 
@@ -218,12 +248,16 @@
     def terms(weights):
         return jnp.dot(weights, ggT[...], preferred_element_type=F32)
 
-    def ra1_copy(d, i):
-        return remote(s1A.at[d, i], t1A.at[d, i], ra1_send.at[d, i], ra1_recv.at[d, i], r, at((z_next, z_last)[d], y, h))
-
-    def rb1_copy(d, i):
-        to = ((y_next, y_last)[d] if d < 2 else (y_next2, y_last2)[i])
-        return remote(s1B.at[d, i], t1B.at[d, i], rb1_send.at[d, i], rb1_recv.at[d, i], r, at(z, to, h))
+    def ra1_copy(d, g):
+        rows = group_a(g)
+        return remote(
+            s1A.at[d, :, rows], t1A.at[d, :, rows], ra1_send.at[d, g], ra1_recv.at[d, g], r, at((z_next, z_last)[d], y, h)
+        )
+
+    def rb1_copy(d, g):
+        rows = group_b(g)
+        src, dst = (s1B.at[d, :, rows], t1B.at[d, :, rows]) if d < 2 else (s1B.at[2, d - 2, rows], t1B.at[2, d - 2, rows])
+        return remote(src, dst, rb1_send.at[d, g], rb1_recv.at[d, g], r, at(z, y_to[d], h))
 
     def ra2_copy(o):
         to = (y + o) % NY
@@ -237,23 +271,28 @@
 
     def ra3_copy(o):
         to = (z + ZG * o) % NZ
-        return remote(v2A.at[to // ZG], t3A.at[o - 1], ra3_send.at[o - 1], ra3_recv.at[o - 1], r, at(to, y, h))
-
-    def rb3_copy():
-        return remote(v2B.at[1 - j], t3B, rb3_send.at[0], rb3_recv.at[0], r, at(z, (y + QY) % NY, h))
+        return remote(v2A.at[to // ZG], t3A.at[h * ROWS + o], ra3_send.at[o], ra3_recv.at[h * ROWS + o], r, at(to, y, 0))
+
+    def rb3_copy(e):
+        to = (y + QY * e) % NY
+        return remote(v2B.at[to // QY], t3B.at[2 * h + e], rb3_send.at[e], rb3_recv.at[2 * h + e], r, at(z, to, 1))
 
     for i in range(2):
-        s1B[2, i] = terms(wB[i, q_far]).astype(BF16)
-        go(rb1_copy(2, i))
+        for d in range(3):
+            s1B[d, i] = terms(wB[i, (q_next, q_last, q_far)[d]]).astype(BF16)
+    for g in (2, 1, 3, 0):
+        for d in (2, 3, 0, 1):
+            go(rb1_copy(d, g))
+    for i in range(ROWS):
         for d in range(2):
             s1A[d, i] = terms(wA[i, (m_next, m_last)[d]]).astype(BF16)
-            go(ra1_copy(d, i))
+    for g in (1, 0):
+        for d in range(2):
+            go(ra1_copy(d, g))
     for i in range(2):
-        for d in range(2):
-            s1B[d, i] = terms(wB[i, (q_next, q_last)[d]]).astype(BF16)
-            go(rb1_copy(d, i))
-            s1A[d, 2 + i] = terms(wA[2 + i, (m_next, m_last)[d]]).astype(BF16)
-            go(ra1_copy(d, 2 + i))
+        u1B[i] = terms(wB[i, q])
+    for i in range(ROWS):
+        u1A[i] = terms(wA[i, m])
 
     owners = (r, sibling, across, diagonal)
 
@@ -281,37 +320,45 @@
             mine[2, i] = (mine[2, i].astype(F32) + other[1, i].astype(F32)).astype(BF16)
         pass_on(2, 2, part, across)
 
+    def add_a(g):
+        rows = group_a(g)
+        for d in range(2):
+            ra1_copy(d, g).wait_recv()
+        total = u1A[:, rows, :] + t1A[0, :, rows, :].astype(F32) + t1A[1, :, rows, :].astype(F32)
+        u1A[:, rows, :] = total
+        v1A[:, rows, :] = total.astype(BF16)
+        for t in (2, 1, 3, 0)[:QY - 1 + g]:
+            to = (j + g) % 2 * QY + (q + t) % QY
+            go(ra2_copy((to + NY - y) % NY))
+
+    def add_b(g):
+        rows = group_b(g)
+        for d in (2, 3, 0, 1):
+            rb1_copy(d, g).wait_recv()
+        total = u1B[:, rows, :]
+        for d in range(3):
+            total += t1B[d, :, rows, :].astype(F32)
+        u1B[:, rows, :] = total
+        v1B[:, rows, :] = total.astype(BF16)
+        for t in (1, 2, 0)[:ZG if g else ZG - 1]:
+            to = (k + g) % ROWS * ZG + (m + t) % ZG
+            go(rb2_copy((to + NZ - z) % NZ))
+
     every = range(NY)
-    for i, slot in ((3, 1), (2, None)):
-        grads_a(i)
-        if slot is not None:
-            pass_on(i, slot, 0, sibling)
-        grads_b(i, every)
-        if slot is not None:
-            pass_on(i, slot, 1, sibling)
-    for i in range(ROWS):
-        u1A[i] = terms(wA[i, m])
-    for i in range(2):
-        u1B[i] = terms(wB[i, q])
+    grads_a(3)
+    pass_on(3, 1, 0, sibling)
+    grads_b(3, every)
+    pass_on(3, 1, 1, sibling)
+    add_b(2)
+    add_a(1)
+    grads_a(2)
+    grads_b(2, every)
+    add_b(1)
     add_sibling(0)
+    add_b(3)
     add_sibling(1)
-
-    for i in range(ROWS):
-        for d in range(2):
-            ra1_copy(d, i).wait_recv()
-        total = u1A[i] + t1A[0, i].astype(F32) + t1A[1, i].astype(F32)
-        u1A[i] = total
-        v1A[i] = total.astype(BF16)
-    for o in FAR_Y:
-        go(ra2_copy(o))
-    for i in range(2):
-        for d in (2, 0, 1):
-            rb1_copy(d, i).wait_recv()
-        total = u1B[i] + t1B[0, i].astype(F32) + t1B[1, i].astype(F32) + t1B[2, i].astype(F32)
-        u1B[i] = total
-        v1B[i] = total.astype(BF16)
-    for o in FAR_Z:
-        go(rb2_copy(o))
+    add_a(0)
+    add_b(0)
 
     grads_a(1)
     pass_on(1, 0, 0, sibling)
@@ -326,25 +373,26 @@
     fin[0:ROWS] = total
     for o in (2, 1, 3):
         go(ra3_copy(o))
+
+    @pl.when(h == 1)
+    def _():
+        ra3_copy(0).start()
+
     total = u1B[:, zb, :]
     for o in FAR_Z[::-1]:
         rb2_copy(o).wait_recv()
         total += t2B[o - 1].astype(F32)
     v2B[...] = total.astype(BF16)
     fin[ROWS:ROWS + 2] = total
-    go(rb3_copy())
+    go(rb3_copy(1))
+
+    @pl.when(h == 0)
+    def _():
+        rb3_copy(0).start()
+
 
     grads_a(0)
     grads_b(0, every)
-
-    total = fin[k]
-    for o in (1, 3, 2):
-        ra3_copy(o).wait_recv()
-        total += t3A[o - 1].astype(F32)
-    fin[ROWS + 2] = total
-    rb3_copy().wait_recv()
-    fin[ROWS + 3] = fin[ROWS + j] + t3B[...].astype(F32)
-    go(remote(fin.at[ROWS + 3 - h], fb, h_send.at[1], h_recv.at[1], r, partner))
 
     def put(row, dw, keep):
         dg_ref[row:row + FEATS, :] = dw[:, :128] * keep
@@ -365,10 +413,48 @@
             dw = dB[0, yy, rows, :].astype(F32) + qB[0, yy, rows, :].astype(F32) + qB[2, yy, rows, :].astype(F32)
             put(((zz * NY + yy) * NH + 1) * FEATS, dw, keep_of(zz, yy))
 
-    arrived(fb, h_recv.at[1], r, partner)
-    ig_ref[...] = (fin[ROWS + 2 + h] + fb[...]).astype(BF16)
+    stores = [
+        pltpu.make_async_copy(src, dst, store_sem.at[i])
+        for i, (src, dst) in enumerate(((hid_ref, hid_hbm), (dg_ref, dg_hbm), (du_ref, du_hbm)))
+    ]
+    for store in stores:
+        store.start()
+
     for copy in sent:
         copy.wait_send()
+
+    @pl.when(h == 0)
+    def _():
+        for copy in first_round(0):
+            copy.wait_send()
+        rb3_copy(0).wait_send()
+
+    @pl.when(h == 1)
+    def _():
+        for copy in first_round(1):
+            copy.wait_send()
+        ra3_copy(0).wait_send()
+
+    @pl.when(h == 0)
+    def _():
+        total = fin[k]
+        for plane, o in ((0, 1), (0, 3), (1, 0), (1, 1), (1, 3), (0, 2), (1, 2)):
+            slot = plane * ROWS + o
+            arrived(t3A.at[slot], ra3_recv.at[slot], r, at((z + NZ - ZG * o) % NZ, y, plane))
+            total += t3A[slot].astype(F32)
+        ig_ref[...] = total.astype(BF16)
+
+    @pl.when(h == 1)
+    def _():
+        total = fin[ROWS + j]
+        for plane, e in ((1, 1), (0, 0), (0, 1)):
+            slot = 2 * plane + e
+            arrived(t3B.at[slot], rb3_recv.at[slot], r, at(z, (y + QY * e) % NY, plane))
+            total += t3B[slot].astype(F32)
+        ig_ref[...] = total.astype(BF16)
+
+    for store in stores:
+        store.wait()
 
 
 def body(tokens, gate_weight, up_weight, block_mask, cotangent):
@@ -384,13 +470,16 @@
             jax.ShapeDtypeStruct(up_weight.shape, F32),
         ),
         in_specs=[vmem, hbm, hbm, pl.BlockSpec(memory_space=pltpu.SMEM), hbm],
-        out_specs=(vmem,) * 4,
+        out_specs=(hbm, vmem, hbm, hbm),
         scratch_shapes=[
+            pltpu.VMEM(cotangent.shape, BF16),
+            pltpu.VMEM(gate_weight.shape, F32),
+            pltpu.VMEM(up_weight.shape, F32),
+            dma((3,)),
             pltpu.VMEM(gate_weight.shape, BF16),
             pltpu.VMEM(up_weight.shape, BF16),
             pltpu.VMEM(cotangent.shape, BF16),
             dma((3,)),
-            pltpu.VMEM((NH, FEATS, TOK), BF16),
             pltpu.VMEM((ROWS, ZG, ROW_A, TOK), BF16),
             pltpu.VMEM((2, QY, ROW_B, TOK), BF16),
             pltpu.VMEM((ROWS, ZG, ROW_A, 256), BF16),
@@ -413,16 +502,17 @@
             pltpu.VMEM((NZ - 1, 2, FEATS, TOK), BF16),
             pltpu.VMEM((ROWS, FEATS, TOK), BF16),
             pltpu.VMEM((2, FEATS, TOK), BF16),
-            pltpu.VMEM((ROWS - 1, FEATS, TOK), BF16),
-            pltpu.VMEM((FEATS, TOK), BF16),
-            pltpu.VMEM((ROWS + 4, FEATS, TOK), F32),
-            pltpu.VMEM((FEATS, TOK), F32),
-            dma((2,)), dma((2,)), dma((3, 2)), dma((3, 2)), dma((3, 2)), dma((3, 2)),
-            *[dma(n) for n in ((ROWS - 1,), (NY - 1,), (2, ROWS), (1,), (NZ - 1,), (3, 2)) for _ in range(2)],
-            *[dma(n) for n in ((2, ROWS), (NY - 1,), (ROWS - 1,), (3, 2), (NZ - 1,), (1,)) for _ in range(2)],
+            pltpu.VMEM((2 * ROWS, FEATS, TOK), BF16),
+            pltpu.VMEM((4, FEATS, TOK), BF16),
+            pltpu.VMEM((ROWS + 2, FEATS, TOK), F32),
+            dma((3, 2)), dma((3, 2)), dma((3, 2)), dma((3, 2)),
+            dma((ROWS, NH)), dma((ROWS,)), dma((NY - 1,)), dma((NY - 1,)), dma((2, 2)), dma((2, 2)),
+            dma((2, NH)), dma((2,)), dma((NZ - 1,)), dma((NZ - 1,)), dma((4, ROWS)), dma((4, ROWS)),
+            dma((2, 2)), dma((2, 2)), dma((NY - 1,)), dma((NY - 1,)), dma((ROWS,)), dma((2 * ROWS,)),
+            dma((4, ROWS)), dma((4, ROWS)), dma((NZ - 1,)), dma((NZ - 1,)), dma((2,)), dma((4,)),
         ],
         compiler_params=pltpu.CompilerParams(
-            collective_id=0, has_side_effects=True, vmem_limit_bytes=40 << 20
+            collective_id=0, has_side_effects=True, vmem_limit_bytes=60 << 20
         ),
     )(tokens.T, gate_weight, up_weight, block_mask.T, cotangent)
     return hidden, input_grad.T, gate_grad, up_grad

time: 80.6 us -> 78.1 us (0.969)
  the two profiles are of different devices: /device:TPU:8 before, /device:TPU:6 now
where the time goes in v4:
time: 78.1 us; the launch traced here: 77.2 us
  Pallas kernels  71.5 us (92%)
  local copies, waits for them, and re-layouts  5 us (6%)
    pallas_call x1, Pallas kernels, body(): pl.pallas_call(kernel, out_shape=(jax.ShapeDtypeStruct(cotangent.shape, B...  71.5 us
    unnamed x8, local copies, waits for them, and re-layouts  5 us

profile of v4, /device:TPU:6, one launch (start us, length us, event | category | flops | bytes accessed | tf_op | source)
XLA Modules:
  0.0 77.2 jit_solution(13381445217674178181)
XLA Ops:
  0.6 71.5 %shard_map.84 = (bf16[128,128]{1,0:T(8,128)(2,1)}, bf16[32,128]{1,0:T(8,128)(2,1)}, f32[1536,128]{1,0:T(8,128)}, f32[1536,128]{1,0:T(8,128)}) custom-call(bf16[32,128]{1,0:T(8,128)(2,1)} %bitcast.3, bf16[1536,128]{1,0:T(8,128)(2,1)} %wg_hbm.1, bf16[1536,128]{1,0:T(8,128)(2,1)} %wu_hbm.1, s32[1,48]{1,0:T(1,128)} %bitcast.5, bf16[128,128]{1,0:T(8,128)(2,1)} %cot_hbm.1), custom_call_target="tpu_custom_call" | custom-call | tf_op jit(solution)/shard_map/pallas_call | solution.py:464
  72.2 0.0 copy-start.1
  72.2 1.4 %copy.13 = bf16[128,128]{1,0:T(8,128)(2,1)} copy(bf16[128,128]{1,0:T(8,128)(2,1)} %get-tuple-element.16) | data formatting | bytes 65536
  73.5 0.0 copy-done.1
  73.5 0.6 copy.14
  74.1 0.0 copy-start
  74.1 2.1 %copy.15 = f32[1536,128]{1,0:T(8,128)} copy(f32[1536,128]{1,0:T(8,128)} %get-tuple-element.18) | data formatting | bytes 1572864
  76.3 0.0 copy-done
  76.3 0.9 %copy.16 = f32[1536,128]{1,0:T(8,128)} copy(f32[1536,128]{1,0:T(8,128)S(1)} %copy-done) | data formatting | bytes 1572864
Async XLA Ops:
  72.2 1.4 %copy-start.1 = (bf16[32,128]{1,0:T(8,128)(2,1)S(1)}, bf16[32,128]{1,0:T(8,128)(2,1)}, u32[]{:S(2)}) copy-start(bf16[32,128]{1,0:T(8,128)(2,1)} %get-tuple-element.9) | copy-start | bytes 24580
  74.1 2.1 %copy-start = (f32[1536,128]{1,0:T(8,128)S(1)}, f32[1536,128]{1,0:T(8,128)}, u32[]{:S(2)}) copy-start(f32[1536,128]{1,0:T(8,128)} %get-tuple-element.19) | copy-start | bytes 2359300

commit v5 on v4

--- a/solution.py
+++ b/solution.py
@@ -134,13 +134,13 @@
             wB.at[:, :, pl.ds(pl.multiple_of(row * GROUP_B, FEATS), GROUP_B)],
         )
 
-    def hand(which, owner, row):
-        for part in range(2):
+    def hand(which, owner, row, parts=(0, 1)):
+        for part in parts:
             ref = weights_of(owner)[part]
             go(remote(ref, ref, w_send.at[which, part], w_recv.at[which, part], row, col))
 
-    def handed(which, owner, row):
-        for part in range(2):
+    def handed(which, owner, row, parts=(0, 1)):
+        for part in parts:
             arrived(weights_of(owner)[part], w_recv.at[which, part], row, col)
 
     hand(1, r, across)
@@ -210,8 +210,9 @@
         (wait_b2 if half else wait_a2)(g)
         for d in (2, 3, 0, 1) if half else (0, 1):
             go((b3_copy if half else a3_copy)(d, g))
-    handed(1, across, across)
-    hand(2, across, sibling)
+    for part in range(2):
+        handed(1, across, across, (part,))
+        hand(2, across, sibling, (part,))
     for half, g in ((0, 0), (1, 0), (1, 1), (1, 3), (0, 1), (1, 2)):
         for d in (2, 3, 0, 1) if half else (0, 1):
             if half:

time: 78.1 us -> 77.8 us (level)
  Pallas kernels: 71.5 us -> 70.6 us
    pallas_call x1, Pallas kernels: 71.5 us -> 70.6 us  [body(): pl.pallas_call(kernel, out_shape=(jax.ShapeDtypeStruct(cotangent.shape, B...]
where the time goes in v5:
time: 77.8 us; the launch traced here: 76.2 us
  Pallas kernels  70.6 us (91%)
  local copies, waits for them, and re-layouts  5 us (6%)
    pallas_call x1, Pallas kernels, body(): pl.pallas_call(kernel, out_shape=(jax.ShapeDtypeStruct(cotangent.shape, B...  70.6 us
    unnamed x8, local copies, waits for them, and re-layouts  5 us

profile of v5, /device:TPU:6, one launch (start us, length us, event | category | flops | bytes accessed | tf_op | source)
XLA Modules:
  0.0 76.2 jit_solution(8311877441482358023)
XLA Ops:
  0.6 70.6 %shard_map.84 = (bf16[128,128]{1,0:T(8,128)(2,1)}, bf16[32,128]{1,0:T(8,128)(2,1)}, f32[1536,128]{1,0:T(8,128)}, f32[1536,128]{1,0:T(8,128)}) custom-call(bf16[32,128]{1,0:T(8,128)(2,1)} %bitcast.3, bf16[1536,128]{1,0:T(8,128)(2,1)} %wg_hbm.1, bf16[1536,128]{1,0:T(8,128)(2,1)} %wu_hbm.1, s32[1,48]{1,0:T(1,128)} %bitcast.5, bf16[128,128]{1,0:T(8,128)(2,1)} %cot_hbm.1), custom_call_target="tpu_custom_call" | custom-call | tf_op jit(solution)/shard_map/pallas_call | solution.py:465
  71.2 0.0 copy-start.1
  71.2 1.4 %copy.13 = bf16[128,128]{1,0:T(8,128)(2,1)} copy(bf16[128,128]{1,0:T(8,128)(2,1)} %get-tuple-element.16) | data formatting | bytes 65536
  72.6 0.0 copy-done.1
  72.6 0.6 copy.14
  73.2 0.0 copy-start
  73.2 2.1 %copy.15 = f32[1536,128]{1,0:T(8,128)} copy(f32[1536,128]{1,0:T(8,128)} %get-tuple-element.18) | data formatting | bytes 1572864
  75.3 0.0 copy-done
  75.4 0.9 %copy.16 = f32[1536,128]{1,0:T(8,128)} copy(f32[1536,128]{1,0:T(8,128)S(1)} %copy-done) | data formatting | bytes 1572864
Async XLA Ops:
  71.2 1.4 %copy-start.1 = (bf16[32,128]{1,0:T(8,128)(2,1)S(1)}, bf16[32,128]{1,0:T(8,128)(2,1)}, u32[]{:S(2)}) copy-start(bf16[32,128]{1,0:T(8,128)(2,1)} %get-tuple-element.9) | copy-start | bytes 24580
  73.2 2.1 %copy-start = (f32[1536,128]{1,0:T(8,128)S(1)}, f32[1536,128]{1,0:T(8,128)}, u32[]{:S(2)}) copy-start(f32[1536,128]{1,0:T(8,128)} %get-tuple-element.19) | copy-start | bytes 2359300
